TPU v7x, 32 devices: a whole 2x2x4 slice. The times are simulated.
32 devices in a mesh: groups: 2 (over y), pix: 16 (over z, x, core).
Axes of the slice: x: 2, y: 2, z: 4, core: 2. Of those that a mesh axis runs over, the one named last changes fastest.
Arguments:
- new_obs: bfloat16 [24, 10, 32768], P(None, None, ('groups', 'pix')), parts along dimension 2, may hold values from -72 to 72
- old_obs: bfloat16 [24, 10, 32768], P(None, None, ('groups', 'pix')), parts along dimension 2, may hold values from -6 to 6
- new_mask: int32 [24, 32768], P(None, ('groups', 'pix')), parts along dimension 1, may hold values 0 or 1
- new_dates: int32 [24], replicated, may hold values from 0 to 1460
- old_dates: int32 [24], replicated, may hold values from 0 to 1460
- kept_gram: float32 [64, 32768], P(None, ('groups', 'pix')), parts along dimension 1, may hold values from -864 to 864, as said below
- kept_rhs: float32 [8, 10, 32768], P(None, None, ('groups', 'pix')), parts along dimension 2, may hold values from -6914 to 6914
Outputs:
- coefficients: float32 [8, 10, 32768], P(None, None, ('groups', 'pix')), parts along dimension 2
- retired: bfloat16 [24, 10, 32768], P(None, None, ('groups', 'pix')), parts along dimension 2
There are 2 independent parts, one for each index of `groups`. A program takes and returns all parts, laid end to end along the dimension named above; an argument that names none is the same for every part. Nothing has to cross between parts.
Inputs may be any that keep to these rules, and one draw needn't show every extreme that they name: For every pixel, kept_gram holds the sums of products of design rows over the valid ones of 216 dates.
All inputs are finite; a program needn't handle non-finite values. No bound on the sum of `new_mask` on one device may be relied on, other than what follows from the above.
Results may differ from a plain program's by a relative error of at most 0.0004.
Values may be sent and summed in bfloat16 or wider, within the bound.
A program may use at most 64 MiB of HBM per device.

v0:
```python
import functools
import math

import jax
import jax.numpy as jnp
from jax import lax
from jax.experimental import pallas as pl
from jax.experimental.pallas import tpu as pltpu
from jax.sharding import PartitionSpec as P

OMEGA = 2.0 * math.pi / 365.25
CENTER = 730.0
YEAR_DAYS = 365.25
RIDGE = 0.5
EPSILON = 1e-06
TERMS = 8
LANES = 128
MESH = pl.DeviceIdType.MESH


def design(day_values):
    moment = day_values.astype(jnp.float32)
    columns = [jnp.ones_like(moment), (moment - CENTER) / YEAR_DAYS]
    for harmonic in range(1, 4):
        columns.append(jnp.cos(harmonic * OMEGA * moment))
        columns.append(jnp.sin(harmonic * OMEGA * moment))
    return jnp.stack(columns, axis=1)


def pair_rows(harmonic_rows):
    count = harmonic_rows.shape[0]
    terms = harmonic_rows.shape[1]
    return (harmonic_rows[:, :, None] * harmonic_rows[:, None, :]).reshape(count, terms * terms)


def cholesky_solve(normal_sums, right_sums):
    terms = right_sums.shape[0]
    factor = {}
    for row_at in range(terms):
        for col_at in range(row_at + 1):
            total = normal_sums[row_at * terms + col_at]
            if row_at == col_at:
                total = total + RIDGE
            for middle in range(col_at):
                total = total - factor[row_at, middle] * factor[col_at, middle]
            if row_at == col_at:
                factor[row_at, row_at] = jnp.sqrt(total)
            else:
                factor[row_at, col_at] = total / factor[col_at, col_at]
    forward = []
    for row_at in range(terms):
        total = right_sums[row_at]
        for middle in range(row_at):
            total = total - factor[row_at, middle][None, :] * forward[middle]
        forward.append(total / factor[row_at, row_at][None, :])
    backward = [None] * terms
    for row_at in reversed(range(terms)):
        total = forward[row_at]
        for middle in range(row_at + 1, terms):
            total = total - factor[middle, row_at][None, :] * backward[middle]
        backward[row_at] = total / factor[row_at, row_at][None, :]
    return jnp.stack(backward)


def plain_on_device(new_obs, old_obs, new_mask, new_dates, old_dates, kept_gram, kept_rhs):
    highest = lax.Precision.HIGHEST
    owners = lax.axis_size("pix")
    dates_count, band_count, local_pix = new_obs.shape
    stride = local_pix // owners

    def split_owner(values):
        return values.reshape(values.shape[0], values.shape[1], owners, stride)

    def join_owner(values):
        return values.reshape(values.shape[0], values.shape[1], local_pix)

    entering = join_owner(
        lax.all_to_all(split_owner(new_obs), "pix", split_axis=2, concat_axis=2, tiled=True)
    )
    enter_rows = design(new_dates)
    leave_rows = design(old_dates)
    weights = new_mask.astype(jnp.float32)
    normal_sums = kept_gram + jnp.einsum(
        "kn,kp->np", pair_rows(enter_rows), weights, precision=highest
    )
    observed = weights[:, None, :] * entering.astype(jnp.float32)
    right_sums = kept_rhs + jnp.einsum("ka,kbp->abp", enter_rows, observed, precision=highest)
    coefficients = cholesky_solve(normal_sums, right_sums)
    fitted = jnp.einsum("ka,abp->kbp", enter_rows, coefficients, precision=highest)
    misfit = weights[:, None, :] * (entering.astype(jnp.float32) - fitted)
    spread = lax.psum(jnp.sum(misfit * misfit, axis=(0, 2)), "pix")
    inverse_spread = 1.0 / jnp.sqrt(spread / (dates_count * local_pix * owners) + EPSILON)
    tile_coefs = join_owner(
        lax.all_to_all(split_owner(coefficients), "pix", split_axis=2, concat_axis=2, tiled=True)
    )
    old_fit = jnp.einsum("ka,abp->kbp", leave_rows, tile_coefs, precision=highest)
    standard = ((old_obs.astype(jnp.float32) - old_fit) * inverse_spread[None, :, None]).astype(
        jnp.bfloat16
    )
    return (coefficients, standard)


def harmonic_values(moment, term):
    slope = (moment - CENTER) / YEAR_DAYS
    rate = jnp.where(
        term < 4,
        jnp.float32(1 * OMEGA),
        jnp.where(term < 6, jnp.float32(2 * OMEGA), jnp.float32(3 * OMEGA)),
    )
    angle = rate * moment
    wave = jnp.where(lax.rem(term, 2) == 0, jnp.cos(angle), jnp.sin(angle))
    return jnp.where(term == 0, 1.0, jnp.where(term == 1, slope, wave))


def narrow(values):
    return values.astype(jnp.bfloat16).astype(jnp.float32)


def three_parts(values):
    high = narrow(values)
    middle = narrow(values - high)
    return high, middle, values - high - middle


def days_along(dates_ref, count, shape, axis):
    at = lax.rem(lax.broadcasted_iota(jnp.int32, shape, axis), count)
    days = jnp.zeros(shape, jnp.int32)
    for date_at in range(count):
        days = jnp.where(at == date_at, dates_ref[date_at], days)
    return days.astype(jnp.float32)


def fit_table(dates_ref, dates_count, bands):
    width = bands * TERMS
    shape = (dates_count, 3 * width)
    days = days_along(dates_ref, dates_count, shape, 0)
    lane = lax.broadcasted_iota(jnp.int32, shape, 1)
    rows = harmonic_values(days, lax.rem(lane, TERMS))
    high = narrow(rows)
    rows = jnp.where(lane < 2 * width, high, rows - high)
    inner = lax.rem(lane, width)
    blocks = [
        jnp.where((inner >= band * TERMS) & (inner < (band + 1) * TERMS), rows, 0.0)
        for band in range(bands)
    ]
    return jnp.concatenate(blocks, axis=0).astype(jnp.bfloat16)


def stacked_parts(coefs):
    high = coefs.astype(jnp.bfloat16)
    low = (coefs - high.astype(jnp.float32)).astype(jnp.bfloat16)
    return jnp.concatenate([high, low, high], axis=0)


def pair_split(first, second, half):
    lane = lax.broadcasted_iota(jnp.int32, first.shape, 1)
    low = jnp.where(lane < half, first, pltpu.roll(second, half, 1))
    high = jnp.where(lane < half, pltpu.roll(first, half, 1), second)
    return low, high


def refit_kernel(
    owners,
    dates_count,
    bands,
    local_pix,
    x_hbm, old_hbm, mask_hbm, new_dates_hbm, old_dates_hbm, gram_hbm, rhs_hbm,
    coef_out, retired_out,
    x_ref, old_ref, mask_ref, gram_ref, rhs_ref, new_dates, old_dates,
    send_x, got_x, send_c, got_c, send_s, got_s,
    inverse_ref, right_table, enter_table, leave_table, square_ref, rest_ref,
    load_sem, x_send_sem, x_recv_sem, c_send_sem, c_recv_sem, s_send_sem, s_recv_sem,
    relay_x, x_relay_sem, x_pass_sem,
):
    dot = lambda a, b: jnp.dot(a, b, preferred_element_type=jnp.float32)
    me = lax.axis_index("pix")
    half = LANES // 2
    tiles = local_pix // LANES
    rows = dates_count * bands
    width = TERMS * bands
    levels = owners.bit_length() - 1

    def flip(base, amount, bits):
        result = 0
        for level in range(bits):
            weight = 1 << level
            result = result + weight * ((base // weight + amount // weight) % 2)
        return result

    loads = [
        pltpu.make_async_copy(source, target, load_sem.at[at])
        for at, (source, target) in enumerate(
            (
                (x_hbm, x_ref), (new_dates_hbm, new_dates), (old_dates_hbm, old_dates),
                (mask_hbm, mask_ref), (gram_hbm, gram_ref), (rhs_hbm, rhs_ref), (old_hbm, old_ref),
            )
        )
    ]
    for load in loads:
        load.start()
    barrier = pltpu.get_barrier_semaphore()
    for offset in range(1, owners):
        pl.semaphore_signal(
            barrier, inc=1, device_id={"pix": flip(me, offset, levels)}, device_id_type=MESH
        )

    loads[0].wait()
    for tile in range(tiles):
        values = x_ref[:, tile * LANES:(tile + 1) * LANES].astype(jnp.float32)
        low, high = pair_split(values[:rows // 2], values[rows // 2:], half)
        send_x[2 * tile] = low.astype(jnp.bfloat16)
        send_x[2 * tile + 1] = high.astype(jnp.bfloat16)
    pl.semaphore_wait(barrier, owners - 1)

    def remote(source, target, send_sem, recv_sem, peer):
        return pltpu.make_async_remote_copy(
            src_ref=source.at[peer],
            dst_ref=target.at[me],
            send_sem=send_sem.at[peer],
            recv_sem=recv_sem.at[me],
            device_id={"pix": peer},
            device_id_type=MESH,
        )

    def arrive(target, recv_sem, peer):
        pltpu.make_async_copy(target.at[peer], target.at[peer], recv_sem.at[peer]).wait()

    quarter = owners // 4
    behind = (me + owners - quarter) % owners
    ahead = (me + quarter) % owners
    x_relayed = range(owners // 2 + owners // 8, owners // 2 + quarter)

    def first_leg(source, relay, send_sem, recv_sem, slot, peer):
        return pltpu.make_async_remote_copy(
            src_ref=source.at[peer],
            dst_ref=relay.at[slot],
            send_sem=send_sem.at[peer],
            recv_sem=recv_sem.at[slot],
            device_id={"pix": behind},
            device_id_type=MESH,
        )

    def second_leg(relay, target, send_sem, recv_sem, slot, offset):
        return pltpu.make_async_remote_copy(
            src_ref=relay.at[slot],
            dst_ref=target.at[ahead],
            send_sem=send_sem.at[slot],
            recv_sem=recv_sem.at[ahead],
            device_id={"pix": flip(ahead, offset, levels)},
            device_id_type=MESH,
        )

    for slot, offset in enumerate(x_relayed):
        first_leg(send_x, relay_x, x_send_sem, x_relay_sem, slot, flip(me, offset, levels)).start()
    for offset in range(1, owners):
        if offset not in x_relayed:
            remote(send_x, got_x, x_send_sem, x_recv_sem, flip(me, offset, levels)).start()
    pltpu.make_async_copy(send_x.at[me], got_x.at[me], x_recv_sem.at[me]).start()

    loads[1].wait()
    loads[2].wait()
    lane = lax.broadcasted_iota(jnp.int32, (TERMS, rows), 1)
    across = harmonic_values(
        days_along(new_dates, dates_count, (TERMS, rows), 1),
        lax.broadcasted_iota(jnp.int32, (TERMS, rows), 0),
    )
    for part_at, part in enumerate(three_parts(across)):
        blocks = [
            jnp.where((lane >= band * dates_count) & (lane < (band + 1) * dates_count), part, 0.0)
            for band in range(bands)
        ]
        right_table[part_at * width:(part_at + 1) * width] = jnp.concatenate(blocks, axis=0).astype(jnp.bfloat16)
    enter_table[...] = fit_table(new_dates, dates_count, bands)
    leave_table[...] = fit_table(old_dates, dates_count, bands)

    for slot, offset in enumerate(x_relayed):
        arrive(relay_x, x_relay_sem, slot)
        second_leg(relay_x, got_x, x_pass_sem, x_recv_sem, slot, offset).start()

    design_rows = across[:, :dates_count]
    paired = jnp.concatenate([design_rows[at:at + 1] * design_rows for at in range(TERMS)], axis=0)
    loads[3].wait()
    loads[4].wait()
    weights = mask_ref[...].astype(jnp.float32).astype(jnp.bfloat16)
    normal = gram_ref[...]
    for part in reversed(three_parts(paired)):
        normal = normal + dot(part.astype(jnp.bfloat16), weights)
    sub = lax.broadcasted_iota(jnp.int32, (TERMS, local_pix), 0)
    matrix = [
        normal[at * TERMS:(at + 1) * TERMS] + jnp.where(sub == at, RIDGE, 0.0) for at in range(TERMS)
    ]
    for pivot in range(TERMS):
        scale = 1.0 / matrix[pivot][pivot:pivot + 1]
        pivot_row = jnp.where(sub == pivot, 1.0, matrix[pivot]) * scale
        for at in range(TERMS):
            if at != pivot:
                matrix[at] = (
                    jnp.where(sub == pivot, 0.0, matrix[at]) - matrix[at][pivot:pivot + 1] * pivot_row
                )
        matrix[pivot] = pivot_row
    for at in range(TERMS):
        inverse_ref[at] = matrix[at]

    square_ref[...] = jnp.zeros_like(square_ref)
    loads[5].wait()

    def tile_at(step):
        far, near = step // quarter, step % quarter
        return flip(me // 2, quarter * far + (near + far * (quarter // 2)) % quarter, levels - 1)

    def own_step(step, carry):
        tile = tile_at(step)
        columns = pl.ds(pl.multiple_of(tile * LANES, LANES), LANES)
        arrive(got_x, x_recv_sem, 2 * tile)
        arrive(got_x, x_recv_sem, 2 * tile + 1)
        low, high = pair_split(
            got_x[2 * tile].astype(jnp.float32), got_x[2 * tile + 1].astype(jnp.float32), half
        )
        entering = jnp.concatenate([low, high], axis=0)
        valid = mask_ref[:, columns].astype(jnp.float32)
        valid = jnp.concatenate([valid] * bands, axis=0)
        parts = dot(right_table[...], (entering * valid).astype(jnp.bfloat16))
        right = (parts[2 * width:] + parts[width:2 * width]) + parts[:width] + rhs_ref[:, columns]
        columns_of = [inverse_ref[at, :, columns] for at in range(TERMS)]
        solved = []
        for band in range(bands):
            total = None
            for at in range(TERMS):
                spot = band * TERMS + at
                term = columns_of[at] * right[spot:spot + 1]
                total = term if total is None else total + term
            solved.append(total)
        coefs = jnp.concatenate(solved, axis=0)
        coef_out[:, columns] = coefs
        low, high = pair_split(coefs[:width // 2], coefs[width // 2:], half)
        send_c[2 * tile] = low
        send_c[2 * tile + 1] = high
        fitted = dot(enter_table[...], stacked_parts(coefs))
        misfit = valid * (entering - fitted)
        square_ref[...] += misfit * misfit

        @pl.when(step > 0)
        def _():
            remote(send_c, got_c, c_send_sem, c_recv_sem, 2 * tile).start()
            remote(send_c, got_c, c_send_sem, c_recv_sem, 2 * tile + 1).start()

        @pl.when(step == 0)
        def _():
            remote(send_c, got_c, c_send_sem, c_recv_sem, flip(me, 1, levels)).start()
            pltpu.make_async_copy(send_c.at[me], got_c.at[me], c_recv_sem.at[me]).start()

        return carry

    lax.fori_loop(0, tiles, own_step, 0)

    spot = lax.broadcasted_iota(jnp.int32, (1, LANES), 1)
    local = jnp.zeros((1, LANES), jnp.float32)
    for band in range(bands):
        total = jnp.sum(square_ref[band * dates_count:(band + 1) * dates_count], axis=0, keepdims=True)
        local = jnp.where(spot == band, jnp.sum(total, axis=1, keepdims=True), local)
    send_s[...] = local

    def spread_copy(peer):
        return pltpu.make_async_remote_copy(
            src_ref=send_s,
            dst_ref=got_s.at[me],
            send_sem=s_send_sem.at[peer],
            recv_sem=s_recv_sem.at[me],
            device_id={"pix": peer},
            device_id_type=MESH,
        )

    for offset in reversed(range(1, owners)):
        spread_copy(flip(me, offset, levels)).start()
    pltpu.make_async_copy(send_s, got_s.at[me], s_recv_sem.at[me]).start()
    loads[6].wait()

    def rest_step(step, carry):
        tile = tile_at(step)
        columns = pl.ds(pl.multiple_of(tile * LANES, LANES), LANES)
        arrive(got_c, c_recv_sem, 2 * tile)
        arrive(got_c, c_recv_sem, 2 * tile + 1)
        low, high = pair_split(got_c[2 * tile], got_c[2 * tile + 1], half)
        fitted = dot(leave_table[...], stacked_parts(jnp.concatenate([low, high], axis=0)))
        rest_ref[:, columns] = old_ref[:, columns].astype(jnp.float32) - fitted
        return carry

    lax.fori_loop(0, tiles, rest_step, 0)

    for peer in range(owners):
        arrive(got_s, s_recv_sem, peer)
    spread = jnp.sum(got_s[...], axis=0) / (dates_count * local_pix * owners)
    inverse_spread = 1.0 / jnp.sqrt(spread + EPSILON)
    for band in range(bands):
        scale = jnp.sum(jnp.where(spot == band, inverse_spread, 0.0), axis=1, keepdims=True)
        band_rows = slice(band * dates_count, (band + 1) * dates_count)
        rest_ref[band_rows] = rest_ref[band_rows] * scale
    retired_out[...] = rest_ref[...].astype(jnp.bfloat16)

    for offset in range(1, owners):
        peer = flip(me, offset, levels)
        remote(send_x, got_x, x_send_sem, x_recv_sem, peer).wait_send()
        remote(send_c, got_c, c_send_sem, c_recv_sem, peer).wait_send()
        spread_copy(peer).wait_send()
    for slot, offset in enumerate(x_relayed):
        second_leg(relay_x, got_x, x_pass_sem, x_recv_sem, slot, offset).wait_send()


def fused_on_device(new_obs, old_obs, new_mask, new_dates, old_dates, kept_gram, kept_rhs):
    owners = lax.axis_size("pix")
    dates_count, bands, local_pix = new_obs.shape
    rows = dates_count * bands
    width = TERMS * bands
    stay = lambda values: pltpu.with_memory_space_constraint(values, pltpu.HBM)
    band_major = lambda values: stay(values.transpose(1, 0, 2).reshape(-1, local_pix))
    hbm = pl.BlockSpec(memory_space=pltpu.HBM)
    vmem = pl.BlockSpec(memory_space=pltpu.VMEM)
    f32, bf16 = jnp.float32, jnp.bfloat16
    dma = pltpu.SemaphoreType.DMA
    coefs, retired = pl.pallas_call(
        functools.partial(refit_kernel, owners, dates_count, bands, local_pix),
        out_shape=(
            jax.ShapeDtypeStruct((width, local_pix), f32),
            jax.ShapeDtypeStruct((rows, local_pix), bf16),
        ),
        in_specs=[hbm] * 7,
        out_specs=(vmem, vmem),
        scratch_shapes=[
            pltpu.VMEM((rows, local_pix), bf16),
            pltpu.VMEM((rows, local_pix), bf16),
            pltpu.VMEM((dates_count, local_pix), jnp.int32),
            pltpu.VMEM((TERMS * TERMS, local_pix), f32),
            pltpu.VMEM((width, local_pix), f32),
            pltpu.SMEM((dates_count,), jnp.int32),
            pltpu.SMEM((dates_count,), jnp.int32),
            pltpu.VMEM((owners, rows // 2, LANES), bf16),
            pltpu.VMEM((owners, rows // 2, LANES), bf16),
            pltpu.VMEM((owners, width // 2, LANES), f32),
            pltpu.VMEM((owners, width // 2, LANES), f32),
            pltpu.VMEM((1, LANES), f32),
            pltpu.VMEM((owners, 1, LANES), f32),
            pltpu.VMEM((TERMS, TERMS, local_pix), f32),
            pltpu.VMEM((3 * width, rows), bf16),
            pltpu.VMEM((rows, 3 * width), bf16),
            pltpu.VMEM((rows, 3 * width), bf16),
            pltpu.VMEM((rows, LANES), f32),
            pltpu.VMEM((rows, local_pix), f32),
            dma((7,)),
            dma((owners,)), dma((owners,)),
            dma((owners,)), dma((owners,)),
            dma((owners,)), dma((owners,)),
            pltpu.VMEM((owners // 8, rows // 2, LANES), bf16),
            dma((owners // 8,)), dma((owners // 8,)),
        ],
        compiler_params=pltpu.CompilerParams(
            collective_id=0, has_side_effects=True, vmem_limit_bytes=20 << 20
        ),
    )(
        band_major(new_obs), band_major(old_obs), stay(new_mask), stay(new_dates), stay(old_dates),
        stay(kept_gram), band_major(kept_rhs),
    )
    return (
        coefs.reshape(bands, TERMS, local_pix).transpose(1, 0, 2),
        retired.reshape(bands, dates_count, local_pix).transpose(1, 0, 2),
    )


def on_device(*arrays):
    owners = lax.axis_size("pix")
    dates_count, bands, local_pix = arrays[0].shape
    fits = (
        local_pix == owners * (LANES // 2)
        and owners >= 8
        and owners & (owners - 1) == 0
        and arrays[6].shape[0] == TERMS
        and dates_count % 8 == 0
        and bands % 2 == 0
    )
    return fused_on_device(*arrays) if fits else plain_on_device(*arrays)


def solution(mesh):
    return jax.shard_map(
        on_device,
        mesh=mesh,
        in_specs=(
            P(None, None, ("groups", "pix")),
            P(None, None, ("groups", "pix")),
            P(None, ("groups", "pix")),
            P(),
            P(),
            P(None, ("groups", "pix")),
            P(None, None, ("groups", "pix")),
        ),
        out_specs=(P(None, None, ("groups", "pix")), P(None, None, ("groups", "pix"))),
        check_vma=False,
    )
```

profile of v0, /device:TPU:0, one launch (start us, length us, event | category | flops | bytes accessed | tf_op | source)
XLA Modules:
  0.0 29.0 jit_solution(4862943440050476738)
XLA Ops:
  0.6 26.9 %shard_map.86 = (f32[80,1024]{1,0:T(8,128)S(1)}, bf16[240,1024]{1,0:T(8,128)(2,1)S(1)}) custom-call(bf16[240,1024]{1,0:T(8,128)(2,1)} %bitcast.17, bf16[240,1024]{1,0:T(8,128)(2,1)} %bitcast.18, s32[24,1024]{1,0:T(8,128)} %mask_hbm.1, s32[24]{0:T(128)} %new_dates_hbm.1, s32[24]{0:T(128)} %old_dates_hbm.1, f32[64,1024]{1,0:T(8,128)} %gram_hbm.1, ...), custom_call_target="tpu_custom_call" | custom-call | tf_op jit(solution)/shard_map/pallas_call | solution.py:420
  27.5 0.7 %copy.11 = f32[8,10,1024]{2,0,1:T(8,128)} copy(f32[8,10,1024]{2,0,1:T(8,128)S(1)} %bitcast.16) | data formatting | bytes 655360
  28.3 0.8 %copy.12 = bf16[24,10,1024]{2,0,1:T(8,128)(2,1)} copy(bf16[24,10,1024]{2,0,1:T(8,128)(2,1)S(1)} %bitcast.15) | data formatting | bytes 983040
where the time goes:
time: 29.2 us; the launch traced here: 29 us
  Pallas kernels  26.9 us (92%)
  local copies, waits for them, and re-layouts  1.5 us (5%)
  between operations  0.64 us (2%)
    pallas_call x1, Pallas kernels, fused_on_device(): pl.pallas_call(functools.partial(refit_kernel, owners, dates_count, bands...  26.9 us
    unnamed x2, local copies, waits for them, and re-layouts  1.5 us

commit v1 on v0

v1 whole, which is shorter than its diff:
```python
import functools
import math

import jax
import jax.numpy as jnp
import numpy as np
from jax import lax
from jax.experimental import pallas as pl
from jax.experimental.pallas import tpu as pltpu
from jax.sharding import PartitionSpec as P

OMEGA = 2.0 * math.pi / 365.25
CENTER = 730.0
YEAR_DAYS = 365.25
RIDGE = 0.5
EPSILON = 1e-06
TERMS = 8
LANES = 128
STEPS = 32767.0
LEVELS = 32.0
SMALLEST = 1e-30
GRAM_ROWS = 11
MESH = pl.DeviceIdType.MESH


def design(day_values):
    moment = day_values.astype(jnp.float32)
    columns = [jnp.ones_like(moment), (moment - CENTER) / YEAR_DAYS]
    for harmonic in range(1, 4):
        columns.append(jnp.cos(harmonic * OMEGA * moment))
        columns.append(jnp.sin(harmonic * OMEGA * moment))
    return jnp.stack(columns, axis=1)


def pair_rows(harmonic_rows):
    count = harmonic_rows.shape[0]
    terms = harmonic_rows.shape[1]
    return (harmonic_rows[:, :, None] * harmonic_rows[:, None, :]).reshape(count, terms * terms)


def cholesky_solve(normal_sums, right_sums):
    terms = right_sums.shape[0]
    factor = {}
    for row_at in range(terms):
        for col_at in range(row_at + 1):
            total = normal_sums[row_at * terms + col_at]
            if row_at == col_at:
                total = total + RIDGE
            for middle in range(col_at):
                total = total - factor[row_at, middle] * factor[col_at, middle]
            if row_at == col_at:
                factor[row_at, row_at] = jnp.sqrt(total)
            else:
                factor[row_at, col_at] = total / factor[col_at, col_at]
    forward = []
    for row_at in range(terms):
        total = right_sums[row_at]
        for middle in range(row_at):
            total = total - factor[row_at, middle][None, :] * forward[middle]
        forward.append(total / factor[row_at, row_at][None, :])
    backward = [None] * terms
    for row_at in reversed(range(terms)):
        total = forward[row_at]
        for middle in range(row_at + 1, terms):
            total = total - factor[middle, row_at][None, :] * backward[middle]
        backward[row_at] = total / factor[row_at, row_at][None, :]
    return jnp.stack(backward)


def plain_on_device(new_obs, old_obs, new_mask, new_dates, old_dates, kept_gram, kept_rhs):
    highest = lax.Precision.HIGHEST
    owners = lax.axis_size("pix")
    dates_count, band_count, local_pix = new_obs.shape
    stride = local_pix // owners

    def split_owner(values):
        return values.reshape(values.shape[0], values.shape[1], owners, stride)

    def join_owner(values):
        return values.reshape(values.shape[0], values.shape[1], local_pix)

    entering = join_owner(
        lax.all_to_all(split_owner(new_obs), "pix", split_axis=2, concat_axis=2, tiled=True)
    )
    enter_rows = design(new_dates)
    leave_rows = design(old_dates)
    weights = new_mask.astype(jnp.float32)
    normal_sums = kept_gram + jnp.einsum(
        "kn,kp->np", pair_rows(enter_rows), weights, precision=highest
    )
    observed = weights[:, None, :] * entering.astype(jnp.float32)
    right_sums = kept_rhs + jnp.einsum("ka,kbp->abp", enter_rows, observed, precision=highest)
    coefficients = cholesky_solve(normal_sums, right_sums)
    fitted = jnp.einsum("ka,abp->kbp", enter_rows, coefficients, precision=highest)
    misfit = weights[:, None, :] * (entering.astype(jnp.float32) - fitted)
    spread = lax.psum(jnp.sum(misfit * misfit, axis=(0, 2)), "pix")
    inverse_spread = 1.0 / jnp.sqrt(spread / (dates_count * local_pix * owners) + EPSILON)
    tile_coefs = join_owner(
        lax.all_to_all(split_owner(coefficients), "pix", split_axis=2, concat_axis=2, tiled=True)
    )
    old_fit = jnp.einsum("ka,abp->kbp", leave_rows, tile_coefs, precision=highest)
    standard = ((old_obs.astype(jnp.float32) - old_fit) * inverse_spread[None, :, None]).astype(
        jnp.bfloat16
    )
    return (coefficients, standard)


def harmonic_values(moment, term):
    slope = (moment - CENTER) / YEAR_DAYS
    rate = jnp.where(
        term < 4,
        jnp.float32(1 * OMEGA),
        jnp.where(term < 6, jnp.float32(2 * OMEGA), jnp.float32(3 * OMEGA)),
    )
    angle = rate * moment
    wave = jnp.where(lax.rem(term, 2) == 0, jnp.cos(angle), jnp.sin(angle))
    return jnp.where(term == 0, 1.0, jnp.where(term == 1, slope, wave))


def narrow(values):
    return values.astype(jnp.bfloat16).astype(jnp.float32)


def three_parts(values):
    high = narrow(values)
    middle = narrow(values - high)
    return high, middle, values - high - middle


def days_along(dates_ref, count, shape, axis):
    at = lax.rem(lax.broadcasted_iota(jnp.int32, shape, axis), count)
    days = jnp.zeros(shape, jnp.int32)
    for date_at in range(count):
        days = jnp.where(at == date_at, dates_ref[date_at], days)
    return days.astype(jnp.float32)


def fit_table(dates_ref, dates_count, bands):
    width = bands * TERMS
    shape = (dates_count, 3 * width)
    days = days_along(dates_ref, dates_count, shape, 0)
    lane = lax.broadcasted_iota(jnp.int32, shape, 1)
    rows = harmonic_values(days, lax.rem(lane, TERMS))
    high = narrow(rows)
    rows = jnp.where(lane < 2 * width, high, rows - high)
    inner = lax.rem(lane, width)
    blocks = [
        jnp.where((inner >= band * TERMS) & (inner < (band + 1) * TERMS), rows, 0.0)
        for band in range(bands)
    ]
    return jnp.concatenate(blocks, axis=0).astype(jnp.bfloat16)


def stacked_parts(coefs):
    high = coefs.astype(jnp.bfloat16)
    low = (coefs - high.astype(jnp.float32)).astype(jnp.bfloat16)
    return jnp.concatenate([high, low, high], axis=0)


def pair_split(first, second, half):
    lane = lax.broadcasted_iota(jnp.int32, first.shape, 1)
    low = jnp.where(lane < half, first, pltpu.roll(second, half, 1))
    high = jnp.where(lane < half, pltpu.roll(first, half, 1), second)
    return low, high


def gram_mix():
    at = {(0, col): col for col in range(TERMS)}
    at.update({(4, 5): 8, (4, 6): 9, (4, 7): 10, (4, 4): GRAM_ROWS, (6, 6): 19, (6, 7): 20})
    at.update({(1, col): GRAM_ROWS + col for col in range(1, TERMS)})
    count = 2 * GRAM_ROWS

    def unit(*entry):
        row = np.zeros(count)
        row[at[entry]] = 1.0
        return row

    cosine = [unit(0, 0), unit(0, 2), unit(0, 4), unit(0, 6)]
    sine = [np.zeros(count), unit(0, 3), unit(0, 5), unit(0, 7)]
    cosine += [2 * unit(4, 4) - cosine[0], 2 * unit(4, 6) - cosine[1], 2 * unit(6, 6) - cosine[0]]
    sine += [2 * unit(4, 5), 2 * unit(4, 7) - sine[1], 2 * unit(6, 7)]
    mix = np.zeros((TERMS, TERMS, count))
    for row in range(TERMS):
        for col in range(row, TERMS):
            if row < 2:
                value = unit(row, col)
            else:
                first, second = row // 2, col // 2
                apart, joint = second - first, first + second
                if row % 2 == 0 and col % 2 == 0:
                    value = (cosine[apart] + cosine[joint]) / 2
                elif row % 2 == 1 and col % 2 == 1:
                    value = (cosine[apart] - cosine[joint]) / 2
                elif row % 2 == 0:
                    value = (sine[joint] + sine[apart]) / 2
                else:
                    value = (sine[joint] - sine[apart]) / 2
            mix[row, col] = mix[col, row] = value
    mix = np.pad(mix.reshape(TERMS * TERMS, count), ((0, 0), (0, -count % 8)))
    return np.concatenate([mix, mix, mix], axis=1)


def code_levels(peak):
    return jnp.ceil(jnp.log2(jnp.maximum(peak, SMALLEST)) * LEVELS)


def level_sizes(code):
    return jnp.exp2(code * (1.0 / LEVELS))


def fixed_point(values):
    groups = values.shape[0] // TERMS
    grouped = values.reshape(groups, TERMS, LANES)
    code = code_levels(jnp.max(jnp.abs(grouped), axis=1))
    per_step = STEPS / level_sizes(code)
    steps = jnp.clip(jnp.round(grouped * per_step[:, None, :]), -STEPS, STEPS)
    return steps.reshape(values.shape), code


def from_fixed_point(steps, code):
    groups = code.shape[0]
    size = level_sizes(code) * (1.0 / STEPS)
    return (steps.reshape(groups, TERMS, LANES) * size[:, None, :]).reshape(steps.shape)


def fixed_rows(width, bands):
    return width // 2 + bands // 2 + bands // 2 % 2


def send_rows(values, bands, half, send_ref, tile):
    width = values.shape[0]
    rows = fixed_rows(width, bands)
    steps, code = fixed_point(values)
    groups = bands // 2
    extra = jnp.zeros((rows - width // 2 - groups, LANES), jnp.float32)
    first = [steps[:width // 2], code[:groups]]
    second = [steps[width // 2:], code[groups:]]
    if extra.shape[0]:
        first.append(extra)
        second.append(extra)
    low, high = pair_split(jnp.concatenate(first, axis=0), jnp.concatenate(second, axis=0), half)
    send_ref[2 * tile] = low.astype(jnp.int32).astype(jnp.int16)
    send_ref[2 * tile + 1] = high.astype(jnp.int32).astype(jnp.int16)


def take_rows(got_ref, width, bands, half, tile):
    groups = bands // 2
    low, high = pair_split(
        got_ref[2 * tile].astype(jnp.int32).astype(jnp.float32),
        got_ref[2 * tile + 1].astype(jnp.int32).astype(jnp.float32),
        half,
    )
    return jnp.concatenate(
        [
            from_fixed_point(part[:width // 2], part[width // 2:width // 2 + groups])
            for part in (low, high)
        ],
        axis=0,
    )


def row_weight(count, trend):
    sub = lax.broadcasted_iota(jnp.int32, (TERMS, count.shape[1]), 0)
    return jnp.where(sub == 0, count + RIDGE, jnp.where(sub == 1, trend + RIDGE, 0.5 * count + RIDGE))


def refit_kernel(
    owners,
    dates_count,
    bands,
    local_pix,
    x_hbm, old_hbm, mask_hbm, new_dates_hbm, old_dates_hbm, gram_hbm, rhs_hbm, mix_hbm,
    coef_out, rest_ref, scale_out,
    x_ref, old_ref, mask_ref, gram_ref, rhs_ref, new_dates, old_dates, mix_ref,
    send_m, got_m, send_k, got_k, send_r, got_r, send_c, got_c, send_s, got_s,
    valid_ref, kept_ref, right_ref, inverse_ref, right_table, fit_tables, square_ref,
    load_sem, send_sem, k_sem, m_sem, r_sem, c_sem, s_sem,
):
    dot = lambda a, b: jnp.dot(a, b, preferred_element_type=jnp.float32)
    me = lax.axis_index("pix")
    half = LANES // 2
    tiles = local_pix // LANES
    rows = dates_count * bands
    width = TERMS * bands
    levels = owners.bit_length() - 1
    M_SEND, K_SEND, R_SEND, C_SEND, S_SEND = range(5)

    def flip(base, amount, bits):
        result = 0
        for level in range(bits):
            weight = 1 << level
            result = result + weight * ((base // weight + amount // weight) % 2)
        return result

    barrier = pltpu.get_barrier_semaphore()
    for offset in range(1, owners):
        pl.semaphore_signal(
            barrier, inc=1, device_id={"pix": flip(me, offset, levels)}, device_id_type=MESH
        )
    taken = [(0, 2 * TERMS), (4 * TERMS, TERMS), (6 * TERMS, TERMS)]
    gram_parts = []
    spot = 0
    for start, count in taken:
        gram_parts.append((gram_hbm.at[pl.ds(start, count)], gram_ref.at[pl.ds(spot, count)]))
        spot += count
    loads = [
        pltpu.make_async_copy(source, target, load_sem.at[at])
        for at, (source, target) in enumerate(
            [(mask_hbm, mask_ref)] + gram_parts + [
                (rhs_hbm, rhs_ref), (new_dates_hbm, new_dates), (old_dates_hbm, old_dates),
                (mix_hbm, mix_ref), (x_hbm, x_ref), (old_hbm, old_ref),
            ]
        )
    ]
    for load in loads:
        load.start()

    def remote(source, target, kind, recv, peer):
        return pltpu.make_async_remote_copy(
            src_ref=source.at[peer],
            dst_ref=target.at[me],
            send_sem=send_sem.at[kind],
            recv_sem=recv,
            device_id={"pix": peer},
            device_id_type=MESH,
        )

    def arrive(target, sem, tile):
        both = target.at[pl.ds(2 * tile, 2)]
        pltpu.make_async_copy(both, both, sem).wait()

    def sent(source, kind):
        others = source.at[pl.ds(1, owners - 1)]
        pltpu.make_async_copy(others, others, send_sem.at[kind]).wait()

    far_first = [*range(owners // 2, owners), *range(owners // 4, owners // 2), *range(1, owners // 4)]
    my_tile = me // 2

    for load in loads[:4]:
        load.wait()
    sub = lax.broadcasted_iota(jnp.int32, (TERMS, LANES), 0)
    for tile in range(tiles):
        columns = slice(tile * LANES, (tile + 1) * LANES)
        first, second = gram_ref[0:TERMS, columns], gram_ref[TERMS:2 * TERMS, columns]
        fourth, sixth = gram_ref[2 * TERMS:3 * TERMS, columns], gram_ref[3 * TERMS:4 * TERMS, columns]
        second = jnp.where(sub == 0, pltpu.roll(fourth, 4, 0), second)
        low, high = pair_split(first, second, half)
        send_k[2 * tile, 0:TERMS] = low
        send_k[2 * tile + 1, 0:TERMS] = high
        low, high = pair_split(pltpu.roll(fourth, 3, 0), pltpu.roll(sixth, 2, 0), half)
        send_k[2 * tile, TERMS:GRAM_ROWS] = low[:GRAM_ROWS - TERMS]
        send_k[2 * tile + 1, TERMS:GRAM_ROWS] = high[:GRAM_ROWS - TERMS]
        valid = mask_ref[:, columns].astype(jnp.float32)
        low, high = pair_split(valid[:dates_count // 2], valid[dates_count // 2:], half)
        send_m[2 * tile] = low.astype(jnp.bfloat16)
        send_m[2 * tile + 1] = high.astype(jnp.bfloat16)
    pl.semaphore_wait(barrier, owners - 1)
    for offset in far_first:
        peer = flip(me, offset, levels)
        remote(send_m, got_m, M_SEND, m_sem.at[my_tile], peer).start()
        remote(send_k, got_k, K_SEND, k_sem.at[0], peer).start()
    pltpu.make_async_copy(send_m.at[me], got_m.at[me], m_sem.at[my_tile]).start()
    pltpu.make_async_copy(send_k.at[me], got_k.at[me], k_sem.at[0]).start()

    loads[4].wait()

    def rhs_step(step, carry):
        tile = flip(my_tile, tiles - 1 - step, levels - 1)
        columns = pl.ds(pl.multiple_of(tile * LANES, LANES), LANES)
        weight = 1.0 / row_weight(gram_ref[0:1, columns], gram_ref[TERMS + 1:TERMS + 2, columns])
        values = rhs_ref[:, columns].reshape(bands, TERMS, LANES) * weight[None]
        send_rows(values.reshape(width, LANES), bands, half, send_r, tile)

        @pl.when(step < tiles - 1)
        def _():
            remote(send_r, got_r, R_SEND, r_sem.at[my_tile], 2 * tile).start()
            remote(send_r, got_r, R_SEND, r_sem.at[my_tile], 2 * tile + 1).start()

        @pl.when(step == tiles - 1)
        def _():
            remote(send_r, got_r, R_SEND, r_sem.at[my_tile], flip(me, 1, levels)).start()
            pltpu.make_async_copy(send_r.at[me], got_r.at[me], r_sem.at[my_tile]).start()

        return carry

    lax.fori_loop(0, tiles, rhs_step, 0)

    loads[5].wait()
    loads[6].wait()
    lane = lax.broadcasted_iota(jnp.int32, (TERMS, rows), 1)
    across = harmonic_values(
        days_along(new_dates, dates_count, (TERMS, rows), 1),
        lax.broadcasted_iota(jnp.int32, (TERMS, rows), 0),
    )
    for part_at, part in enumerate(three_parts(across)):
        blocks = [
            jnp.where((lane >= band * dates_count) & (lane < (band + 1) * dates_count), part, 0.0)
            for band in range(bands)
        ]
        right_table[part_at * width:(part_at + 1) * width] = jnp.concatenate(blocks, axis=0).astype(jnp.bfloat16)
    fit_tables[0:rows] = fit_table(new_dates, dates_count, bands)
    fit_tables[rows:2 * rows] = fit_table(old_dates, dates_count, bands)
    design_rows = across[:, :dates_count]
    paired = jnp.concatenate([design_rows[at:at + 1] * design_rows for at in range(TERMS)], axis=0)
    square_ref[...] = jnp.zeros_like(square_ref)
    kept_ref[...] = jnp.zeros_like(kept_ref)

    loads[7].wait()
    loads[8].wait()

    def right_step(step, carry):
        tile = flip(my_tile, step, levels - 1)
        columns = pl.ds(pl.multiple_of(tile * LANES, LANES), LANES)
        arrive(got_m, m_sem.at[tile], tile)
        low, high = pair_split(
            got_m[2 * tile].astype(jnp.float32), got_m[2 * tile + 1].astype(jnp.float32), half
        )
        valid_ref[0:dates_count // 2, columns] = low
        valid_ref[dates_count // 2:dates_count, columns] = high
        valid = jnp.concatenate([valid_ref[:, columns]] * bands, axis=0)
        entering = x_ref[:, columns].astype(jnp.float32)
        parts = dot(right_table[...], (entering * valid).astype(jnp.bfloat16))
        right_ref[:, columns] = (parts[2 * width:] + parts[width:2 * width]) + parts[:width]
        return carry

    lax.fori_loop(0, tiles, right_step, 0)

    pltpu.make_async_copy(got_k, got_k, k_sem.at[0]).wait()
    for tile in range(tiles):
        columns = slice(tile * LANES, (tile + 1) * LANES)
        low, high = pair_split(got_k[2 * tile], got_k[2 * tile + 1], half)
        kept_ref[0:GRAM_ROWS, columns] = low
        kept_ref[GRAM_ROWS:2 * GRAM_ROWS, columns] = high
    weights = valid_ref[...].astype(jnp.bfloat16)
    normal = dot(mix_ref[...], jnp.concatenate(three_parts(kept_ref[...]), axis=0).astype(jnp.bfloat16))
    for part in reversed(three_parts(paired)):
        normal = normal + dot(part.astype(jnp.bfloat16), weights)
    sub = lax.broadcasted_iota(jnp.int32, (TERMS, local_pix), 0)
    matrix = [
        normal[at * TERMS:(at + 1) * TERMS] + jnp.where(sub == at, RIDGE, 0.0) for at in range(TERMS)
    ]
    for pivot in range(TERMS):
        scale = 1.0 / matrix[pivot][pivot:pivot + 1]
        pivot_row = jnp.where(sub == pivot, 1.0, matrix[pivot]) * scale
        for at in range(TERMS):
            if at != pivot:
                matrix[at] = (
                    jnp.where(sub == pivot, 0.0, matrix[at]) - matrix[at][pivot:pivot + 1] * pivot_row
                )
        matrix[pivot] = pivot_row
    for at in range(TERMS):
        inverse_ref[at] = matrix[at]

    loads[9].wait()

    def own_step(step, carry):
        tile = flip(my_tile, step, levels - 1)
        columns = pl.ds(pl.multiple_of(tile * LANES, LANES), LANES)
        arrive(got_r, r_sem.at[tile], tile)
        weight = row_weight(kept_ref[0:1, columns], kept_ref[GRAM_ROWS + 1:GRAM_ROWS + 2, columns])
        kept = take_rows(got_r, width, bands, half, tile).reshape(bands, TERMS, LANES) * weight[None]
        right = right_ref[:, columns] + kept.reshape(width, LANES)
        columns_of = [inverse_ref[at, :, columns] for at in range(TERMS)]
        solved = []
        for band in range(bands):
            total = None
            for at in range(TERMS):
                place = band * TERMS + at
                term = columns_of[at] * right[place:place + 1]
                total = term if total is None else total + term
            solved.append(total)
        coefs = jnp.concatenate(solved, axis=0)
        send_rows(coefs, bands, half, send_c, tile)

        @pl.when(step > 0)
        def _():
            remote(send_c, got_c, C_SEND, c_sem.at[my_tile], 2 * tile).start()
            remote(send_c, got_c, C_SEND, c_sem.at[my_tile], 2 * tile + 1).start()

        @pl.when(step == 0)
        def _():
            remote(send_c, got_c, C_SEND, c_sem.at[my_tile], flip(me, 1, levels)).start()
            pltpu.make_async_copy(send_c.at[me], got_c.at[me], c_sem.at[my_tile]).start()

        fitted = dot(fit_tables[...], stacked_parts(coefs))
        valid = jnp.concatenate([valid_ref[:, columns]] * bands, axis=0)
        misfit = valid * (x_ref[:, columns].astype(jnp.float32) - fitted[:rows])
        square_ref[...] += misfit * misfit
        rest_ref[:, columns] = old_ref[:, columns].astype(jnp.float32) - fitted[rows:]
        return carry

    lax.fori_loop(0, tiles, own_step, 0)

    spot = lax.broadcasted_iota(jnp.int32, (1, LANES), 1)
    local = jnp.zeros((1, LANES), jnp.float32)
    for band in range(bands):
        total = jnp.sum(square_ref[band * dates_count:(band + 1) * dates_count], axis=0, keepdims=True)
        local = jnp.where(spot == band, jnp.sum(total, axis=1, keepdims=True), local)
    send_s[...] = local

    def spread_copy(peer):
        return pltpu.make_async_remote_copy(
            src_ref=send_s,
            dst_ref=got_s.at[me],
            send_sem=send_sem.at[S_SEND],
            recv_sem=s_sem.at[0],
            device_id={"pix": peer},
            device_id_type=MESH,
        )

    for offset in far_first:
        spread_copy(flip(me, offset, levels)).start()
    pltpu.make_async_copy(send_s, got_s.at[me], s_sem.at[0]).start()


    def coef_step(step, carry):
        tile = flip(my_tile, step, levels - 1)
        columns = pl.ds(pl.multiple_of(tile * LANES, LANES), LANES)
        arrive(got_c, c_sem.at[tile], tile)
        coef_out[:, columns] = take_rows(got_c, width, bands, half, tile)
        return carry

    lax.fori_loop(0, tiles, coef_step, 0)

    pltpu.make_async_copy(got_s, got_s, s_sem.at[0]).wait()
    spread = jnp.sum(got_s[...], axis=0) / (dates_count * local_pix * owners)
    scale_out[...] = 1.0 / jnp.sqrt(spread + EPSILON)

    sent(send_m, M_SEND)
    sent(send_k, K_SEND)
    sent(send_r, R_SEND)
    sent(send_c, C_SEND)
    sent(got_s, S_SEND)


def finish_kernel(dates_count, bands, coef_ref, rest_ref, scale_ref, coef_hbm, retired_hbm, retired_ref, sems):
    coef_copy = pltpu.make_async_copy(coef_ref, coef_hbm, sems.at[bands])
    coef_copy.start()
    spot = lax.broadcasted_iota(jnp.int32, (1, LANES), 1)
    inverse_spread = scale_ref[...]
    copies = []
    for band in range(bands):
        scale = jnp.sum(jnp.where(spot == band, inverse_spread, 0.0), axis=1, keepdims=True)
        band_rows = slice(band * dates_count, (band + 1) * dates_count)
        retired_ref[band] = (rest_ref[band_rows] * scale).astype(jnp.bfloat16)
        copies.append(pltpu.make_async_copy(retired_ref.at[band], retired_hbm.at[band], sems.at[band]))
        copies[-1].start()
    for copy in copies:
        copy.wait()
    coef_copy.wait()


def fused_on_device(new_obs, old_obs, new_mask, new_dates, old_dates, kept_gram, kept_rhs):
    owners = lax.axis_size("pix")
    dates_count, bands, local_pix = new_obs.shape
    rows = dates_count * bands
    width = TERMS * bands
    tiles = local_pix // LANES
    packed = fixed_rows(width, bands)
    stay = lambda values: pltpu.with_memory_space_constraint(values, pltpu.HBM)
    band_major = lambda values: stay(values.transpose(1, 0, 2).reshape(-1, local_pix))
    hbm = pl.BlockSpec(memory_space=pltpu.HBM)
    vmem = pl.BlockSpec(memory_space=pltpu.VMEM)
    f32, bf16, i16 = jnp.float32, jnp.bfloat16, jnp.int16
    dma = pltpu.SemaphoreType.DMA
    mix = jnp.asarray(gram_mix(), bf16)
    coefs, rest, scale = pl.pallas_call(
        functools.partial(refit_kernel, owners, dates_count, bands, local_pix),
        out_shape=(
            pltpu.VMEM((width, local_pix), f32),
            pltpu.VMEM((rows, local_pix), f32),
            pltpu.VMEM((1, LANES), f32),
        ),
        in_specs=[hbm] * 8,
        out_specs=(vmem,) * 3,
        scratch_shapes=[
            pltpu.VMEM((rows, local_pix), bf16),
            pltpu.VMEM((rows, local_pix), bf16),
            pltpu.VMEM((dates_count, local_pix), jnp.int32),
            pltpu.VMEM((4 * TERMS, local_pix), f32),
            pltpu.VMEM((width, local_pix), f32),
            pltpu.SMEM((dates_count,), jnp.int32),
            pltpu.SMEM((dates_count,), jnp.int32),
            pltpu.VMEM(mix.shape, bf16),
            pltpu.VMEM((owners, dates_count // 2, LANES), bf16),
            pltpu.VMEM((owners, dates_count // 2, LANES), bf16),
            pltpu.VMEM((owners, GRAM_ROWS, LANES), f32),
            pltpu.VMEM((owners, GRAM_ROWS, LANES), f32),
            pltpu.VMEM((owners, packed, LANES), i16),
            pltpu.VMEM((owners, packed, LANES), i16),
            pltpu.VMEM((owners, packed, LANES), i16),
            pltpu.VMEM((owners, packed, LANES), i16),
            pltpu.VMEM((1, LANES), f32),
            pltpu.VMEM((owners, 1, LANES), f32),
            pltpu.VMEM((dates_count, local_pix), f32),
            pltpu.VMEM((mix.shape[1] // 3, local_pix), f32),
            pltpu.VMEM((width, local_pix), f32),
            pltpu.VMEM((TERMS, TERMS, local_pix), f32),
            pltpu.VMEM((3 * width, rows), bf16),
            pltpu.VMEM((2 * rows, 3 * width), bf16),
            pltpu.VMEM((rows, LANES), f32),
            dma((10,)), dma((5,)), dma((1,)), dma((tiles,)), dma((tiles,)), dma((tiles,)), dma((1,)),
        ],
        compiler_params=pltpu.CompilerParams(
            collective_id=0, has_side_effects=True, vmem_limit_bytes=20 << 20
        ),
    )(
        band_major(new_obs), band_major(old_obs), stay(new_mask), stay(new_dates), stay(old_dates),
        stay(kept_gram), band_major(kept_rhs), stay(mix),
    )
    coefs, retired = pl.pallas_call(
        functools.partial(finish_kernel, dates_count, bands),
        out_shape=(
            jax.ShapeDtypeStruct((width, local_pix), f32),
            jax.ShapeDtypeStruct((bands, dates_count, local_pix), bf16),
        ),
        in_specs=[vmem] * 3,
        out_specs=(hbm, hbm),
        scratch_shapes=[pltpu.VMEM((bands, dates_count, local_pix), bf16), dma((bands + 1,))],
        compiler_params=pltpu.CompilerParams(vmem_limit_bytes=4 << 20),
    )(coefs, rest, scale)
    return (
        coefs.reshape(bands, TERMS, local_pix).transpose(1, 0, 2),
        retired.transpose(1, 0, 2),
    )


def on_device(*arrays):
    owners = lax.axis_size("pix")
    dates_count, bands, local_pix = arrays[0].shape
    fits = (
        local_pix == owners * (LANES // 2)
        and owners >= 8
        and owners & (owners - 1) == 0
        and arrays[6].shape[0] == TERMS
        and dates_count % 8 == 0
        and bands % 2 == 0
    )
    return fused_on_device(*arrays) if fits else plain_on_device(*arrays)


def solution(mesh):
    return jax.shard_map(
        on_device,
        mesh=mesh,
        in_specs=(
            P(None, None, ("groups", "pix")),
            P(None, None, ("groups", "pix")),
            P(None, ("groups", "pix")),
            P(),
            P(),
            P(None, ("groups", "pix")),
            P(None, None, ("groups", "pix")),
        ),
        out_specs=(P(None, None, ("groups", "pix")), P(None, None, ("groups", "pix"))),
        check_vma=False,
    )
```

time: 29.2 us -> 25.5 us (0.87)
  Pallas kernels: 26.9 us -> 24.7 us
  local copies, waits for them, and re-layouts: 1.5 us -> 0 us
    pallas_call x1, Pallas kernels: 26.9 us -> 23.8 us  [fused_on_device(): pl.pallas_call(functools.partial(refit_kernel, owners, dates_count, bands...]
    unnamed x2 -> x0, local copies, waits for them, and re-layouts: 1.5 us -> none
    pallas_call x0 -> x1, Pallas kernels: none -> 0.97 us  [fused_on_device(): pl.pallas_call(functools.partial(finish_kernel, dates_count, bands), out_...]
where the time goes in v1:
time: 25.5 us; the launch traced here: 25.4 us
  Pallas kernels  24.7 us (97%)
  between operations  0.64 us (3%)
    pallas_call x1, Pallas kernels, fused_on_device(): pl.pallas_call(functools.partial(refit_kernel, owners, dates_count, bands...  23.8 us
    pallas_call x1, Pallas kernels, fused_on_device(): pl.pallas_call(functools.partial(finish_kernel, dates_count, bands), out_...  0.97 us

profile of v1, /device:TPU:0, one launch (start us, length us, event | category | flops | bytes accessed | tf_op | source)
XLA Modules:
  0.0 25.4 jit_solution(4426725106428536695)
XLA Ops:
  0.6 23.8 %shard_map.95 = (f32[80,1024]{1,0:T(8,128)S(1)}, f32[240,1024]{1,0:T(8,128)S(1)}, f32[1,128]{1,0:T(1,128)S(1)}) custom-call(bf16[240,1024]{1,0:T(8,128)(2,1)} %bitcast.13, bf16[240,1024]{1,0:T(8,128)(2,1)} %bitcast.14, s32[24,1024]{1,0:T(8,128)} %mask_hbm.1, s32[24]{0:T(128)} %new_dates_hbm.1, s32[24]{0:T(128)} %old_dates_hbm.1, f32[64,1024]{1,0:T(8,128)} %gram_hbm.1, ...), custom_call_target="tpu_custom_call" | custom-call | tf_op jit(solution)/shard_map/pallas_call | solution.py:567
  24.4 1.0 %shard_map.96 = (f32[80,1024]{1,0:T(8,128)}, bf16[10,24,1024]{2,1,0:T(8,128)(2,1)}) custom-call(f32[80,1024]{1,0:T(8,128)S(1)} %get-tuple-element.7.coef_ref, f32[240,1024]{1,0:T(8,128)S(1)} %get-tuple-element.8.rest_ref, f32[1,128]{1,0:T(1,128)S(1)} %get-tuple-element.9.scale_ref), custom_call_target="tpu_custom_call" | custom-call | tf_op jit(solution)/shard_map/pallas_call | solution.py:611

commit v2 on v1

--- a/solution.py
+++ b/solution.py
@@ -135,28 +135,6 @@
     return days.astype(jnp.float32)
 
 
-def fit_table(dates_ref, dates_count, bands):
-    width = bands * TERMS
-    shape = (dates_count, 3 * width)
-    days = days_along(dates_ref, dates_count, shape, 0)
-    lane = lax.broadcasted_iota(jnp.int32, shape, 1)
-    rows = harmonic_values(days, lax.rem(lane, TERMS))
-    high = narrow(rows)
-    rows = jnp.where(lane < 2 * width, high, rows - high)
-    inner = lax.rem(lane, width)
-    blocks = [
-        jnp.where((inner >= band * TERMS) & (inner < (band + 1) * TERMS), rows, 0.0)
-        for band in range(bands)
-    ]
-    return jnp.concatenate(blocks, axis=0).astype(jnp.bfloat16)
-
-
-def stacked_parts(coefs):
-    high = coefs.astype(jnp.bfloat16)
-    low = (coefs - high.astype(jnp.float32)).astype(jnp.bfloat16)
-    return jnp.concatenate([high, low, high], axis=0)
-
-
 def pair_split(first, second, half):
     lane = lax.broadcasted_iota(jnp.int32, first.shape, 1)
     low = jnp.where(lane < half, first, pltpu.roll(second, half, 1))
@@ -212,7 +190,7 @@
     groups = values.shape[0] // TERMS
     grouped = values.reshape(groups, TERMS, LANES)
     code = code_levels(jnp.max(jnp.abs(grouped), axis=1))
-    per_step = STEPS / level_sizes(code)
+    per_step = STEPS * level_sizes(-code)
     steps = jnp.clip(jnp.round(grouped * per_step[:, None, :]), -STEPS, STEPS)
     return steps.reshape(values.shape), code
 
@@ -264,6 +242,15 @@
     return jnp.where(sub == 0, count + RIDGE, jnp.where(sub == 1, trend + RIDGE, 0.5 * count + RIDGE))
 
 
+def fit_rows(dates_ref, dates_count):
+    shape = (dates_count, 3 * TERMS)
+    days = days_along(dates_ref, dates_count, shape, 0)
+    lane = lax.broadcasted_iota(jnp.int32, shape, 1)
+    rows = harmonic_values(days, lax.rem(lane, TERMS))
+    high = narrow(rows)
+    return jnp.where(lane < 2 * TERMS, high, rows - high)
+
+
 def refit_kernel(
     owners,
     dates_count,
@@ -273,17 +260,23 @@
     coef_out, rest_ref, scale_out,
     x_ref, old_ref, mask_ref, gram_ref, rhs_ref, new_dates, old_dates, mix_ref,
     send_m, got_m, send_k, got_k, send_r, got_r, send_c, got_c, send_s, got_s,
-    valid_ref, kept_ref, right_ref, inverse_ref, right_table, fit_tables, square_ref,
+    valid_ref, kept_ref, square_ref,
     load_sem, send_sem, k_sem, m_sem, r_sem, c_sem, s_sem,
 ):
     dot = lambda a, b: jnp.dot(a, b, preferred_element_type=jnp.float32)
     me = lax.axis_index("pix")
     half = LANES // 2
     tiles = local_pix // LANES
-    rows = dates_count * bands
     width = TERMS * bands
     levels = owners.bit_length() - 1
     M_SEND, K_SEND, R_SEND, C_SEND, S_SEND = range(5)
+    NEAR, FAR, LAST = range(3)
+    units = [
+        list(range(tiles // 2)),
+        list(range(tiles // 2, tiles // 2 + tiles // 4)),
+        list(range(tiles // 2 + tiles // 4, tiles)),
+    ]
+    unit_of = {step: unit for unit, steps in enumerate(units) for step in steps}
 
     def flip(base, amount, bits):
         result = 0
@@ -291,6 +284,15 @@
             weight = 1 << level
             result = result + weight * ((base // weight + amount // weight) % 2)
         return result
+
+    def peers_of(step):
+        return [
+            (flip(me, offset, levels), offset) for offset in (2 * step, 2 * step + 1) if offset
+        ]
+
+    my_tile = me // 2
+    tile_at = [flip(my_tile, step, levels - 1) for step in range(tiles)]
+    columns_at = [pl.ds(pl.multiple_of(tile * LANES, LANES), LANES) for tile in tile_at]
 
     barrier = pltpu.get_barrier_semaphore()
     for offset in range(1, owners):
@@ -325,16 +327,14 @@
             device_id_type=MESH,
         )
 
-    def arrive(target, sem, tile):
-        both = target.at[pl.ds(2 * tile, 2)]
-        pltpu.make_async_copy(both, both, sem).wait()
+    def arrive(target, sems, unit):
+        count = 2 * len(units[unit]) - (unit == NEAR)
+        part = target.at[pl.ds(0, count)]
+        pltpu.make_async_copy(part, part, sems.at[unit]).wait()
 
     def sent(source, kind):
         others = source.at[pl.ds(1, owners - 1)]
         pltpu.make_async_copy(others, others, send_sem.at[kind]).wait()
-
-    far_first = [*range(owners // 2, owners), *range(owners // 4, owners // 2), *range(1, owners // 4)]
-    my_tile = me // 2
 
     for load in loads[:4]:
         load.wait()
@@ -355,174 +355,166 @@
         send_m[2 * tile] = low.astype(jnp.bfloat16)
         send_m[2 * tile + 1] = high.astype(jnp.bfloat16)
     pl.semaphore_wait(barrier, owners - 1)
-    for offset in far_first:
-        peer = flip(me, offset, levels)
-        remote(send_m, got_m, M_SEND, m_sem.at[my_tile], peer).start()
-        remote(send_k, got_k, K_SEND, k_sem.at[0], peer).start()
-    pltpu.make_async_copy(send_m.at[me], got_m.at[me], m_sem.at[my_tile]).start()
-    pltpu.make_async_copy(send_k.at[me], got_k.at[me], k_sem.at[0]).start()
-
+    def send_normal(unit):
+        for step in units[unit]:
+            for peer, _ in peers_of(step):
+                remote(send_m, got_m, M_SEND, m_sem.at[unit], peer).start()
+                remote(send_k, got_k, K_SEND, k_sem.at[unit], peer).start()
+
+    def send_right(unit):
+        for step in units[unit]:
+            columns = columns_at[step]
+            weight = 1.0 / row_weight(gram_ref[0:1, columns], gram_ref[TERMS + 1:TERMS + 2, columns])
+            values = rhs_ref[:, columns].reshape(bands, TERMS, LANES) * weight[None]
+            send_rows(values.reshape(width, LANES), bands, half, send_r, tile_at[step])
+        for step in units[unit]:
+            for peer, _ in peers_of(step):
+                remote(send_r, got_r, R_SEND, r_sem.at[unit], peer).start()
+
+    send_normal(FAR)
+    send_normal(NEAR)
     loads[4].wait()
-
-    def rhs_step(step, carry):
-        tile = flip(my_tile, tiles - 1 - step, levels - 1)
-        columns = pl.ds(pl.multiple_of(tile * LANES, LANES), LANES)
-        weight = 1.0 / row_weight(gram_ref[0:1, columns], gram_ref[TERMS + 1:TERMS + 2, columns])
-        values = rhs_ref[:, columns].reshape(bands, TERMS, LANES) * weight[None]
-        send_rows(values.reshape(width, LANES), bands, half, send_r, tile)
-
-        @pl.when(step < tiles - 1)
-        def _():
-            remote(send_r, got_r, R_SEND, r_sem.at[my_tile], 2 * tile).start()
-            remote(send_r, got_r, R_SEND, r_sem.at[my_tile], 2 * tile + 1).start()
-
-        @pl.when(step == tiles - 1)
-        def _():
-            remote(send_r, got_r, R_SEND, r_sem.at[my_tile], flip(me, 1, levels)).start()
-            pltpu.make_async_copy(send_r.at[me], got_r.at[me], r_sem.at[my_tile]).start()
-
-        return carry
-
-    lax.fori_loop(0, tiles, rhs_step, 0)
+    send_right(FAR)
+    send_right(NEAR)
+    send_normal(LAST)
+    send_right(LAST)
+    got_m[me] = send_m[me]
+    got_k[me] = send_k[me]
+    got_r[me] = send_r[me]
 
     loads[5].wait()
     loads[6].wait()
-    lane = lax.broadcasted_iota(jnp.int32, (TERMS, rows), 1)
     across = harmonic_values(
-        days_along(new_dates, dates_count, (TERMS, rows), 1),
-        lax.broadcasted_iota(jnp.int32, (TERMS, rows), 0),
-    )
-    for part_at, part in enumerate(three_parts(across)):
-        blocks = [
-            jnp.where((lane >= band * dates_count) & (lane < (band + 1) * dates_count), part, 0.0)
-            for band in range(bands)
-        ]
-        right_table[part_at * width:(part_at + 1) * width] = jnp.concatenate(blocks, axis=0).astype(jnp.bfloat16)
-    fit_tables[0:rows] = fit_table(new_dates, dates_count, bands)
-    fit_tables[rows:2 * rows] = fit_table(old_dates, dates_count, bands)
-    design_rows = across[:, :dates_count]
-    paired = jnp.concatenate([design_rows[at:at + 1] * design_rows for at in range(TERMS)], axis=0)
+        days_along(new_dates, dates_count, (TERMS, dates_count), 1),
+        lax.broadcasted_iota(jnp.int32, (TERMS, dates_count), 0),
+    )
+    paired = jnp.concatenate([across[at:at + 1] * across for at in range(TERMS)], axis=0)
+    right_table = jnp.concatenate(three_parts(across), axis=0).astype(jnp.bfloat16)
+    pair_table = jnp.concatenate(three_parts(paired), axis=0).astype(jnp.bfloat16)
+    fit_table = jnp.concatenate(
+        [fit_rows(new_dates, dates_count), fit_rows(old_dates, dates_count)], axis=0
+    ).astype(jnp.bfloat16)
     square_ref[...] = jnp.zeros_like(square_ref)
     kept_ref[...] = jnp.zeros_like(kept_ref)
-
     loads[7].wait()
     loads[8].wait()
-
-    def right_step(step, carry):
-        tile = flip(my_tile, step, levels - 1)
-        columns = pl.ds(pl.multiple_of(tile * LANES, LANES), LANES)
-        arrive(got_m, m_sem.at[tile], tile)
-        low, high = pair_split(
-            got_m[2 * tile].astype(jnp.float32), got_m[2 * tile + 1].astype(jnp.float32), half
-        )
-        valid_ref[0:dates_count // 2, columns] = low
-        valid_ref[dates_count // 2:dates_count, columns] = high
-        valid = jnp.concatenate([valid_ref[:, columns]] * bands, axis=0)
-        entering = x_ref[:, columns].astype(jnp.float32)
-        parts = dot(right_table[...], (entering * valid).astype(jnp.bfloat16))
-        right_ref[:, columns] = (parts[2 * width:] + parts[width:2 * width]) + parts[:width]
-        return carry
-
-    lax.fori_loop(0, tiles, right_step, 0)
-
-    pltpu.make_async_copy(got_k, got_k, k_sem.at[0]).wait()
-    for tile in range(tiles):
-        columns = slice(tile * LANES, (tile + 1) * LANES)
-        low, high = pair_split(got_k[2 * tile], got_k[2 * tile + 1], half)
-        kept_ref[0:GRAM_ROWS, columns] = low
-        kept_ref[GRAM_ROWS:2 * GRAM_ROWS, columns] = high
-    weights = valid_ref[...].astype(jnp.bfloat16)
-    normal = dot(mix_ref[...], jnp.concatenate(three_parts(kept_ref[...]), axis=0).astype(jnp.bfloat16))
-    for part in reversed(three_parts(paired)):
-        normal = normal + dot(part.astype(jnp.bfloat16), weights)
-    sub = lax.broadcasted_iota(jnp.int32, (TERMS, local_pix), 0)
-    matrix = [
-        normal[at * TERMS:(at + 1) * TERMS] + jnp.where(sub == at, RIDGE, 0.0) for at in range(TERMS)
-    ]
-    for pivot in range(TERMS):
-        scale = 1.0 / matrix[pivot][pivot:pivot + 1]
-        pivot_row = jnp.where(sub == pivot, 1.0, matrix[pivot]) * scale
-        for at in range(TERMS):
-            if at != pivot:
-                matrix[at] = (
-                    jnp.where(sub == pivot, 0.0, matrix[at]) - matrix[at][pivot:pivot + 1] * pivot_row
+    loads[9].wait()
+
+    def solve_unit(unit):
+        steps = units[unit]
+        arrive(got_m, m_sem, unit)
+        arrive(got_k, k_sem, unit)
+        arrive(got_r, r_sem, unit)
+        squares = None
+        kepts, valids = [], []
+        for step in steps:
+            tile, columns = tile_at[step], columns_at[step]
+            low, high = pair_split(got_k[2 * tile], got_k[2 * tile + 1], half)
+            kept_ref[0:GRAM_ROWS, columns] = low
+            kept_ref[GRAM_ROWS:2 * GRAM_ROWS, columns] = high
+            low, high = pair_split(
+                got_m[2 * tile].astype(jnp.float32), got_m[2 * tile + 1].astype(jnp.float32), half
+            )
+            valid_ref[0:dates_count // 2, columns] = low
+            valid_ref[dates_count // 2:dates_count, columns] = high
+        kepts = [kept_ref[:, columns_at[step]] for step in steps]
+        valids = [valid_ref[:, columns_at[step]] for step in steps]
+        kept = jnp.concatenate(kepts, axis=1)
+        weights = jnp.concatenate(valids, axis=1).astype(jnp.bfloat16)
+        pairs = dot(pair_table, weights)
+        size = TERMS * TERMS
+        normal = dot(mix_ref[...], jnp.concatenate(three_parts(kept), axis=0).astype(jnp.bfloat16))
+        normal = normal + ((pairs[2 * size:] + pairs[size:2 * size]) + pairs[:size])
+        wide = lax.broadcasted_iota(jnp.int32, (TERMS, LANES * len(steps)), 0)
+        matrix = [
+            normal[at * TERMS:(at + 1) * TERMS] + jnp.where(wide == at, RIDGE, 0.0)
+            for at in range(TERMS)
+        ]
+        for pivot in range(TERMS):
+            scale = 1.0 / matrix[pivot][pivot:pivot + 1]
+            pivot_row = jnp.where(wide == pivot, 1.0, matrix[pivot]) * scale
+            for at in range(TERMS):
+                if at != pivot:
+                    matrix[at] = (
+                        jnp.where(wide == pivot, 0.0, matrix[at]) - matrix[at][pivot:pivot + 1] * pivot_row
+                    )
+            matrix[pivot] = pivot_row
+        for place, step in enumerate(steps):
+            tile, columns = tile_at[step], columns_at[step]
+            valid = valids[place]
+            entering = x_ref[:, columns].astype(jnp.float32)
+            by_band = [
+                entering[band * dates_count:(band + 1) * dates_count] for band in range(bands)
+            ]
+            observed = jnp.concatenate([values * valid for values in by_band], axis=1)
+            parts = dot(right_table, observed.astype(jnp.bfloat16))
+            parts = (parts[2 * TERMS:] + parts[TERMS:2 * TERMS]) + parts[:TERMS]
+            weight = row_weight(kepts[place][0:1], kepts[place][GRAM_ROWS + 1:GRAM_ROWS + 2])
+            kept_rows = take_rows(got_r, width, bands, half, tile)
+            inner = slice(place * LANES, (place + 1) * LANES)
+            solved = []
+            for band in range(bands):
+                right = (
+                    parts[:, band * LANES:(band + 1) * LANES]
+                    + kept_rows[band * TERMS:(band + 1) * TERMS] * weight
                 )
-        matrix[pivot] = pivot_row
-    for at in range(TERMS):
-        inverse_ref[at] = matrix[at]
-
-    loads[9].wait()
-
-    def own_step(step, carry):
-        tile = flip(my_tile, step, levels - 1)
-        columns = pl.ds(pl.multiple_of(tile * LANES, LANES), LANES)
-        arrive(got_r, r_sem.at[tile], tile)
-        weight = row_weight(kept_ref[0:1, columns], kept_ref[GRAM_ROWS + 1:GRAM_ROWS + 2, columns])
-        kept = take_rows(got_r, width, bands, half, tile).reshape(bands, TERMS, LANES) * weight[None]
-        right = right_ref[:, columns] + kept.reshape(width, LANES)
-        columns_of = [inverse_ref[at, :, columns] for at in range(TERMS)]
-        solved = []
-        for band in range(bands):
-            total = None
-            for at in range(TERMS):
-                place = band * TERMS + at
-                term = columns_of[at] * right[place:place + 1]
-                total = term if total is None else total + term
-            solved.append(total)
-        coefs = jnp.concatenate(solved, axis=0)
-        send_rows(coefs, bands, half, send_c, tile)
-
-        @pl.when(step > 0)
-        def _():
-            remote(send_c, got_c, C_SEND, c_sem.at[my_tile], 2 * tile).start()
-            remote(send_c, got_c, C_SEND, c_sem.at[my_tile], 2 * tile + 1).start()
-
-        @pl.when(step == 0)
-        def _():
-            remote(send_c, got_c, C_SEND, c_sem.at[my_tile], flip(me, 1, levels)).start()
-            pltpu.make_async_copy(send_c.at[me], got_c.at[me], c_sem.at[my_tile]).start()
-
-        fitted = dot(fit_tables[...], stacked_parts(coefs))
-        valid = jnp.concatenate([valid_ref[:, columns]] * bands, axis=0)
-        misfit = valid * (x_ref[:, columns].astype(jnp.float32) - fitted[:rows])
-        square_ref[...] += misfit * misfit
-        rest_ref[:, columns] = old_ref[:, columns].astype(jnp.float32) - fitted[rows:]
-        return carry
-
-    lax.fori_loop(0, tiles, own_step, 0)
+                total = None
+                for at in range(TERMS):
+                    term = matrix[at][:, inner] * right[at:at + 1]
+                    total = term if total is None else total + term
+                solved.append(total)
+            send_rows(jnp.concatenate(solved, axis=0), bands, half, send_c, tile)
+            for peer, _ in peers_of(step):
+                remote(send_c, got_c, C_SEND, c_sem.at[unit], peer).start()
+            coefs = jnp.concatenate(solved, axis=1)
+            high = narrow(coefs)
+            stacked = jnp.concatenate([high, coefs - high, high], axis=0).astype(jnp.bfloat16)
+            fitted = dot(fit_table, stacked)
+            for band in range(bands):
+                lanes = slice(band * LANES, (band + 1) * LANES)
+                misfit = valid * (by_band[band] - fitted[:dates_count, lanes])
+                square = misfit * misfit
+                total = square[0:TERMS]
+                for start in range(TERMS, dates_count, TERMS):
+                    total = total + square[start:start + TERMS]
+                square_ref[band * TERMS:(band + 1) * TERMS] += total
+                band_rows = slice(band * dates_count, (band + 1) * dates_count)
+                rest_ref[band_rows, columns] = (
+                    old_ref[band_rows, columns].astype(jnp.float32) - fitted[dates_count:, lanes]
+                )
+        if unit == NEAR:
+            got_c[me] = send_c[me]
+
+    solve_unit(NEAR)
+    solve_unit(FAR)
+    solve_unit(LAST)
 
     spot = lax.broadcasted_iota(jnp.int32, (1, LANES), 1)
     local = jnp.zeros((1, LANES), jnp.float32)
     for band in range(bands):
-        total = jnp.sum(square_ref[band * dates_count:(band + 1) * dates_count], axis=0, keepdims=True)
+        total = jnp.sum(square_ref[band * TERMS:(band + 1) * TERMS], axis=0, keepdims=True)
         local = jnp.where(spot == band, jnp.sum(total, axis=1, keepdims=True), local)
     send_s[...] = local
-
-    def spread_copy(peer):
-        return pltpu.make_async_remote_copy(
-            src_ref=send_s,
-            dst_ref=got_s.at[me],
-            send_sem=send_sem.at[S_SEND],
-            recv_sem=s_sem.at[0],
-            device_id={"pix": peer},
-            device_id_type=MESH,
-        )
-
-    for offset in far_first:
-        spread_copy(flip(me, offset, levels)).start()
-    pltpu.make_async_copy(send_s, got_s.at[me], s_sem.at[0]).start()
-
-
-    def coef_step(step, carry):
-        tile = flip(my_tile, step, levels - 1)
-        columns = pl.ds(pl.multiple_of(tile * LANES, LANES), LANES)
-        arrive(got_c, c_sem.at[tile], tile)
-        coef_out[:, columns] = take_rows(got_c, width, bands, half, tile)
-        return carry
-
-    lax.fori_loop(0, tiles, coef_step, 0)
-
-    pltpu.make_async_copy(got_s, got_s, s_sem.at[0]).wait()
+    got_s[me] = local
+    for unit in (FAR, LAST, NEAR):
+        for step in units[unit]:
+            for peer, _ in peers_of(step):
+                pltpu.make_async_remote_copy(
+                    src_ref=send_s,
+                    dst_ref=got_s.at[me],
+                    send_sem=send_sem.at[S_SEND],
+                    recv_sem=s_sem.at[0],
+                    device_id={"pix": peer},
+                    device_id_type=MESH,
+                ).start()
+
+    for unit in (NEAR, FAR, LAST):
+        arrive(got_c, c_sem, unit)
+        for step in units[unit]:
+            coef_out[:, columns_at[step]] = take_rows(got_c, width, bands, half, tile_at[step])
+
+    others = got_s.at[pl.ds(1, owners - 1)]
+    pltpu.make_async_copy(others, others, s_sem.at[0]).wait()
     spread = jnp.sum(got_s[...], axis=0) / (dates_count * local_pix * owners)
     scale_out[...] = 1.0 / jnp.sqrt(spread + EPSILON)
 
@@ -594,12 +586,8 @@
             pltpu.VMEM((owners, 1, LANES), f32),
             pltpu.VMEM((dates_count, local_pix), f32),
             pltpu.VMEM((mix.shape[1] // 3, local_pix), f32),
-            pltpu.VMEM((width, local_pix), f32),
-            pltpu.VMEM((TERMS, TERMS, local_pix), f32),
-            pltpu.VMEM((3 * width, rows), bf16),
-            pltpu.VMEM((2 * rows, 3 * width), bf16),
-            pltpu.VMEM((rows, LANES), f32),
-            dma((10,)), dma((5,)), dma((1,)), dma((tiles,)), dma((tiles,)), dma((tiles,)), dma((1,)),
+            pltpu.VMEM((width, LANES), f32),
+            dma((10,)), dma((5,)), dma((3,)), dma((3,)), dma((3,)), dma((3,)), dma((1,)),
         ],
         compiler_params=pltpu.CompilerParams(
             collective_id=0, has_side_effects=True, vmem_limit_bytes=20 << 20

time: 25.5 us -> 23.3 us (0.914)
  Pallas kernels: 24.7 us -> 22.5 us
    pallas_call x1, Pallas kernels: 23.8 us -> 21.6 us  [fused_on_device(): pl.pallas_call(functools.partial(refit_kernel, owners, dates_count, bands...]
where the time goes in v2:
time: 23.3 us; the launch traced here: 23.2 us
  Pallas kernels  22.5 us (97%)
  between operations  0.64 us (3%)
    pallas_call x1, Pallas kernels, fused_on_device(): pl.pallas_call(functools.partial(refit_kernel, owners, dates_count, bands...  21.6 us
    pallas_call x1, Pallas kernels, fused_on_device(): pl.pallas_call(functools.partial(finish_kernel, dates_count, bands), out_...  0.97 us

profile of v2, /device:TPU:0, one launch (start us, length us, event | category | flops | bytes accessed | tf_op | source)
XLA Modules:
  0.0 23.2 jit_solution(200758024623684356)
XLA Ops:
  0.6 21.6 %shard_map.95 = (f32[80,1024]{1,0:T(8,128)S(1)}, f32[240,1024]{1,0:T(8,128)S(1)}, f32[1,128]{1,0:T(1,128)S(1)}) custom-call(bf16[240,1024]{1,0:T(8,128)(2,1)} %bitcast.13, bf16[240,1024]{1,0:T(8,128)(2,1)} %bitcast.14, s32[24,1024]{1,0:T(8,128)} %mask_hbm.1, s32[24]{0:T(128)} %new_dates_hbm.1, s32[24]{0:T(128)} %old_dates_hbm.1, f32[64,1024]{1,0:T(8,128)} %gram_hbm.1, ...), custom_call_target="tpu_custom_call" | custom-call | tf_op jit(solution)/shard_map/pallas_call | solution.py:559
  22.2 1.0 %shard_map.96 = (f32[80,1024]{1,0:T(8,128)}, bf16[10,24,1024]{2,1,0:T(8,128)(2,1)}) custom-call(f32[80,1024]{1,0:T(8,128)S(1)} %get-tuple-element.7.coef_ref, f32[240,1024]{1,0:T(8,128)S(1)} %get-tuple-element.8.rest_ref, f32[1,128]{1,0:T(1,128)S(1)} %get-tuple-element.9.scale_ref), custom_call_target="tpu_custom_call" | custom-call | tf_op jit(solution)/shard_map/pallas_call | solution.py:599

commit v3 on v2

v3 whole, which is shorter than its diff:
```python
import functools
import math

import jax
import jax.numpy as jnp
import numpy as np
from jax import lax
from jax.experimental import pallas as pl
from jax.experimental.pallas import tpu as pltpu
from jax.sharding import PartitionSpec as P

OMEGA = 2.0 * math.pi / 365.25
CENTER = 730.0
YEAR_DAYS = 365.25
RIDGE = 0.5
EPSILON = 1e-06
TERMS = 8
LANES = 128
STEPS = 32767.0
SMALLEST = 1e-30
GRAM_ROWS = 11
MESH = pl.DeviceIdType.MESH


def design(day_values):
    moment = day_values.astype(jnp.float32)
    columns = [jnp.ones_like(moment), (moment - CENTER) / YEAR_DAYS]
    for harmonic in range(1, 4):
        columns.append(jnp.cos(harmonic * OMEGA * moment))
        columns.append(jnp.sin(harmonic * OMEGA * moment))
    return jnp.stack(columns, axis=1)


def pair_rows(harmonic_rows):
    count = harmonic_rows.shape[0]
    terms = harmonic_rows.shape[1]
    return (harmonic_rows[:, :, None] * harmonic_rows[:, None, :]).reshape(count, terms * terms)


def cholesky_solve(normal_sums, right_sums):
    terms = right_sums.shape[0]
    factor = {}
    for row_at in range(terms):
        for col_at in range(row_at + 1):
            total = normal_sums[row_at * terms + col_at]
            if row_at == col_at:
                total = total + RIDGE
            for middle in range(col_at):
                total = total - factor[row_at, middle] * factor[col_at, middle]
            if row_at == col_at:
                factor[row_at, row_at] = jnp.sqrt(total)
            else:
                factor[row_at, col_at] = total / factor[col_at, col_at]
    forward = []
    for row_at in range(terms):
        total = right_sums[row_at]
        for middle in range(row_at):
            total = total - factor[row_at, middle][None, :] * forward[middle]
        forward.append(total / factor[row_at, row_at][None, :])
    backward = [None] * terms
    for row_at in reversed(range(terms)):
        total = forward[row_at]
        for middle in range(row_at + 1, terms):
            total = total - factor[middle, row_at][None, :] * backward[middle]
        backward[row_at] = total / factor[row_at, row_at][None, :]
    return jnp.stack(backward)


def plain_on_device(new_obs, old_obs, new_mask, new_dates, old_dates, kept_gram, kept_rhs):
    highest = lax.Precision.HIGHEST
    owners = lax.axis_size("pix")
    dates_count, band_count, local_pix = new_obs.shape
    stride = local_pix // owners

    def split_owner(values):
        return values.reshape(values.shape[0], values.shape[1], owners, stride)

    def join_owner(values):
        return values.reshape(values.shape[0], values.shape[1], local_pix)

    entering = join_owner(
        lax.all_to_all(split_owner(new_obs), "pix", split_axis=2, concat_axis=2, tiled=True)
    )
    enter_rows = design(new_dates)
    leave_rows = design(old_dates)
    weights = new_mask.astype(jnp.float32)
    normal_sums = kept_gram + jnp.einsum(
        "kn,kp->np", pair_rows(enter_rows), weights, precision=highest
    )
    observed = weights[:, None, :] * entering.astype(jnp.float32)
    right_sums = kept_rhs + jnp.einsum("ka,kbp->abp", enter_rows, observed, precision=highest)
    coefficients = cholesky_solve(normal_sums, right_sums)
    fitted = jnp.einsum("ka,abp->kbp", enter_rows, coefficients, precision=highest)
    misfit = weights[:, None, :] * (entering.astype(jnp.float32) - fitted)
    spread = lax.psum(jnp.sum(misfit * misfit, axis=(0, 2)), "pix")
    inverse_spread = 1.0 / jnp.sqrt(spread / (dates_count * local_pix * owners) + EPSILON)
    tile_coefs = join_owner(
        lax.all_to_all(split_owner(coefficients), "pix", split_axis=2, concat_axis=2, tiled=True)
    )
    old_fit = jnp.einsum("ka,abp->kbp", leave_rows, tile_coefs, precision=highest)
    standard = ((old_obs.astype(jnp.float32) - old_fit) * inverse_spread[None, :, None]).astype(
        jnp.bfloat16
    )
    return (coefficients, standard)


def harmonic_values(moment, term):
    slope = (moment - CENTER) / YEAR_DAYS
    rate = jnp.where(
        term < 4,
        jnp.float32(1 * OMEGA),
        jnp.where(term < 6, jnp.float32(2 * OMEGA), jnp.float32(3 * OMEGA)),
    )
    angle = rate * moment
    wave = jnp.where(lax.rem(term, 2) == 0, jnp.cos(angle), jnp.sin(angle))
    return jnp.where(term == 0, 1.0, jnp.where(term == 1, slope, wave))


def narrow(values):
    return values.astype(jnp.bfloat16).astype(jnp.float32)


def three_parts(values):
    high = narrow(values)
    middle = narrow(values - high)
    return high, middle, values - high - middle


def days_along(dates_ref, count, shape, axis):
    at = lax.rem(lax.broadcasted_iota(jnp.int32, shape, axis), count)
    days = jnp.zeros(shape, jnp.int32)
    for date_at in range(count):
        days = jnp.where(at == date_at, dates_ref[date_at], days)
    return days.astype(jnp.float32)


def pair_split(first, second, half):
    lane = lax.broadcasted_iota(jnp.int32, first.shape, 1)
    low = jnp.where(lane < half, first, pltpu.roll(second, half, 1))
    high = jnp.where(lane < half, pltpu.roll(first, half, 1), second)
    return low, high


def gram_mix():
    at = {(0, col): col for col in range(TERMS)}
    at.update({(4, 5): 8, (4, 6): 9, (4, 7): 10, (4, 4): GRAM_ROWS, (6, 6): 19, (6, 7): 20})
    at.update({(1, col): GRAM_ROWS + col for col in range(1, TERMS)})
    count = 2 * GRAM_ROWS

    def unit(*entry):
        row = np.zeros(count)
        row[at[entry]] = 1.0
        return row

    cosine = [unit(0, 0), unit(0, 2), unit(0, 4), unit(0, 6)]
    sine = [np.zeros(count), unit(0, 3), unit(0, 5), unit(0, 7)]
    cosine += [2 * unit(4, 4) - cosine[0], 2 * unit(4, 6) - cosine[1], 2 * unit(6, 6) - cosine[0]]
    sine += [2 * unit(4, 5), 2 * unit(4, 7) - sine[1], 2 * unit(6, 7)]
    mix = np.zeros((TERMS, TERMS, count))
    for row in range(TERMS):
        for col in range(row, TERMS):
            if row < 2:
                value = unit(row, col)
            else:
                first, second = row // 2, col // 2
                apart, joint = second - first, first + second
                if row % 2 == 0 and col % 2 == 0:
                    value = (cosine[apart] + cosine[joint]) / 2
                elif row % 2 == 1 and col % 2 == 1:
                    value = (cosine[apart] - cosine[joint]) / 2
                elif row % 2 == 0:
                    value = (sine[joint] + sine[apart]) / 2
                else:
                    value = (sine[joint] - sine[apart]) / 2
            mix[row, col] = mix[col, row] = value
    mix = np.pad(mix.reshape(TERMS * TERMS, count), ((0, 0), (0, -count % 8)))
    return np.concatenate([mix, mix, mix], axis=1)


def half_peaks(peak, half):
    lane = lax.broadcasted_iota(jnp.int32, peak.shape, 1)
    low = jnp.max(jnp.where(lane < half, peak, 0.0), axis=1, keepdims=True)
    high = jnp.max(jnp.where(lane < half, 0.0, peak), axis=1, keepdims=True)
    return jnp.maximum(jnp.where(lane < half, low, high), SMALLEST)


def lanes_of(column, half):
    lane = lax.broadcasted_iota(jnp.int32, column.shape, 1)
    row = lax.broadcasted_iota(jnp.int32, column.shape, 0)
    return jnp.sum(jnp.where(lax.rem(lane, half) == row, column, 0.0), axis=0, keepdims=True)


def bands_of(first, second, bands, half):
    lane = lax.broadcasted_iota(jnp.int32, (bands, LANES), 1)
    row = lax.broadcasted_iota(jnp.int32, (bands, LANES), 0)
    low = jnp.sum(jnp.where(lane == row, first, 0.0), axis=1, keepdims=True)
    high = jnp.sum(jnp.where(lane == row, second, 0.0), axis=1, keepdims=True)
    return jnp.where(lane < half, low, high)


def send_steps(grouped, size, half, send_ref, tile):
    steps = jnp.round(grouped * (STEPS / size)[:, None, :])
    steps = steps.reshape(-1, LANES)
    middle = steps.shape[0] // 2
    low, high = pair_split(steps[:middle], steps[middle:], half)
    send_ref[2 * tile] = low.astype(jnp.int32).astype(jnp.int16)
    send_ref[2 * tile + 1] = high.astype(jnp.int32).astype(jnp.int16)


def take_steps(got_ref, half, tile):
    low, high = pair_split(
        got_ref[2 * tile].astype(jnp.int32).astype(jnp.float32),
        got_ref[2 * tile + 1].astype(jnp.int32).astype(jnp.float32),
        half,
    )
    return jnp.concatenate([low, high], axis=0).reshape(-1, TERMS, LANES)


def row_weight(count, trend):
    sub = lax.broadcasted_iota(jnp.int32, (TERMS, count.shape[1]), 0)
    return jnp.where(sub == 0, count + RIDGE, jnp.where(sub == 1, trend + RIDGE, 0.5 * count + RIDGE))


def fit_rows(dates_ref, dates_count):
    shape = (dates_count, 3 * TERMS)
    days = days_along(dates_ref, dates_count, shape, 0)
    lane = lax.broadcasted_iota(jnp.int32, shape, 1)
    rows = harmonic_values(days, lax.rem(lane, TERMS))
    high = narrow(rows)
    return jnp.where(lane < 2 * TERMS, high, rows - high)


def refit_kernel(
    owners,
    dates_count,
    bands,
    local_pix,
    x_hbm, old_hbm, mask_hbm, new_dates_hbm, old_dates_hbm, gram_hbm, rhs_hbm, mix_hbm,
    coef_out, rest_ref, scale_out,
    pixels_ref, mask_ref, gram_ref, rhs_ref, new_dates, old_dates, mix_ref,
    send_m, got_m, send_k, got_k, send_r, got_r, send_c, got_c, send_u, got_u, send_s, got_s,
    valid_ref, kept_ref, size_ref, inverse_ref, right_ref, square_ref,
    load_sem, send_sem, k_sem, m_sem, r_sem, c_sem, u_sem, s_sem,
):
    dot = lambda a, b: jnp.dot(a, b, preferred_element_type=jnp.float32)
    me = lax.axis_index("pix")
    half = LANES // 2
    tiles = local_pix // LANES
    width = TERMS * bands
    levels = owners.bit_length() - 1
    x_ref, old_ref = pixels_ref.at[0], pixels_ref.at[1]
    M_SEND, K_SEND, R_SEND, C_SEND, U_SEND, S_SEND = range(6)
    NEAR, FAR, LAST = range(3)
    near_steps = list(range(tiles // 2))
    far_steps = list(range(tiles // 2, tiles))
    units = [near_steps, far_steps[:tiles // 4], far_steps[tiles // 4:]]

    def flip(base, amount, bits):
        result = 0
        for level in range(bits):
            weight = 1 << level
            result = result + weight * ((base // weight + amount // weight) % 2)
        return result

    my_tile = me // 2
    my_half = my_tile // (tiles // 2)
    my_quarter = my_tile // (tiles // 4) % 2
    far_unit = 1 + (my_half + my_quarter) % 2

    def tile_of(step):
        if step in near_steps:
            return flip(my_tile, step, levels - 1)
        place = step - tiles // 2
        return my_half * place + (1 - my_half) * (tiles - 1 - place)

    tile_at = [tile_of(step) for step in range(tiles)]
    columns_at = [pl.ds(pl.multiple_of(tile * LANES, LANES), LANES) for tile in tile_at]

    def peers_of(step):
        if step == 0:
            return [flip(me, 1, levels)]
        return [2 * tile_at[step], 2 * tile_at[step] + 1]

    barrier = pltpu.get_barrier_semaphore()
    for step in reversed(range(tiles)):
        for peer in peers_of(step):
            pl.semaphore_signal(barrier, inc=1, device_id={"pix": peer}, device_id_type=MESH)

    def load(source, target, at):
        copy = pltpu.make_async_copy(source, target, load_sem.at[at])
        copy.start()
        return copy

    mask_load = load(mask_hbm, mask_ref, 0)
    spot = 0
    for start, count in [(0, 2 * TERMS), (4 * TERMS, TERMS), (6 * TERMS, TERMS)]:
        load(gram_hbm.at[pl.ds(start, count)], gram_ref.at[pl.ds(spot, count)], 1)
        spot += count
    rhs_load = load(rhs_hbm, rhs_ref, 2)
    table_loads = [
        load(new_dates_hbm, new_dates, 3), load(old_dates_hbm, old_dates, 4), load(mix_hbm, mix_ref, 5)
    ]
    load(x_hbm, x_ref, 6)
    load(old_hbm, old_ref, 6)

    def remote(source, target, kind, recv, peer):
        return pltpu.make_async_remote_copy(
            src_ref=source.at[peer],
            dst_ref=target.at[me],
            send_sem=send_sem.at[kind],
            recv_sem=recv,
            device_id={"pix": peer},
            device_id_type=MESH,
        )

    def arrive(target, sem, steps):
        part = target.at[pl.ds(0, 2 * len(steps) - (0 in steps))]
        pltpu.make_async_copy(part, part, sem).wait()

    def sent(source, kind):
        others = source.at[pl.ds(1, owners - 1)]
        pltpu.make_async_copy(others, others, send_sem.at[kind]).wait()

    mask_load.wait()
    pltpu.make_async_copy(gram_ref, gram_ref, load_sem.at[1]).wait()
    rhs_load.wait()
    sub = lax.broadcasted_iota(jnp.int32, (TERMS, LANES), 0)
    for tile in range(tiles):
        columns = slice(tile * LANES, (tile + 1) * LANES)
        first, second = gram_ref[0:TERMS, columns], gram_ref[TERMS:2 * TERMS, columns]
        fourth, sixth = gram_ref[2 * TERMS:3 * TERMS, columns], gram_ref[3 * TERMS:4 * TERMS, columns]
        grouped = rhs_ref[:, columns].reshape(bands, TERMS, LANES)
        grouped = grouped * (1.0 / row_weight(first[0:1], second[1:2]))[None]
        peak = jnp.max(jnp.abs(grouped), axis=1)
        size = narrow(half_peaks(peak, half) * 1.01)
        share = jnp.max(peak / size, axis=0, keepdims=True)
        send_steps(grouped, jnp.maximum(size * share, SMALLEST), half, send_r, tile)
        second = jnp.where(sub == 0, pltpu.roll(fourth, 4, 0), second)
        low, high = pair_split(first, second, half)
        send_k[2 * tile, 0:TERMS] = low
        send_k[2 * tile + 1, 0:TERMS] = high
        sixth = jnp.where(sub == GRAM_ROWS - TERMS - 1, share, pltpu.roll(sixth, 2, 0))
        low, high = pair_split(pltpu.roll(fourth, 3, 0), sixth, half)
        send_k[2 * tile, TERMS:GRAM_ROWS] = low[:GRAM_ROWS - TERMS]
        send_k[2 * tile + 1, TERMS:GRAM_ROWS] = high[:GRAM_ROWS - TERMS]
        valid = mask_ref[:, columns].astype(jnp.float32)
        low, high = pair_split(valid[:dates_count // 2], valid[dates_count // 2:], half)
        sizes = lanes_of(size, half)
        send_m[2 * tile] = jnp.concatenate([low, sizes], axis=0).astype(jnp.bfloat16)
        send_m[2 * tile + 1] = jnp.concatenate([high, pltpu.roll(sizes, half, 1)], axis=0).astype(jnp.bfloat16)
    pl.semaphore_wait(barrier, owners - 1)

    def send_normal(steps):
        kind = int(steps[0] in far_steps)
        for step in steps:
            for peer in peers_of(step):
                remote(send_m, got_m, M_SEND, m_sem.at[kind], peer).start()
                remote(send_k, got_k, K_SEND, k_sem.at[kind], peer).start()

    def send_right(steps):
        unit = far_unit if steps[0] in far_steps else NEAR
        for step in steps:
            for peer in peers_of(step):
                remote(send_r, got_r, R_SEND, r_sem.at[unit], peer).start()

    send_normal(far_steps)
    send_normal(near_steps)
    send_right(near_steps)
    send_right(far_steps)
    got_m[me] = send_m[me]
    got_k[me] = send_k[me]
    got_r[me] = send_r[me]

    for table_load in table_loads:
        table_load.wait()
    across = harmonic_values(
        days_along(new_dates, dates_count, (TERMS, dates_count), 1),
        lax.broadcasted_iota(jnp.int32, (TERMS, dates_count), 0),
    )
    paired = jnp.concatenate([across[at:at + 1] * across for at in range(TERMS)], axis=0)
    right_table = jnp.concatenate(three_parts(across), axis=0).astype(jnp.bfloat16)
    pair_table = jnp.concatenate(three_parts(paired), axis=0).astype(jnp.bfloat16)
    enter_table = fit_rows(new_dates, dates_count).astype(jnp.bfloat16)
    leave_table = fit_rows(old_dates, dates_count).astype(jnp.bfloat16)
    square_ref[...] = jnp.zeros_like(square_ref)
    kept_ref[...] = jnp.zeros_like(kept_ref)
    pltpu.make_async_copy(pixels_ref, pixels_ref, load_sem.at[6]).wait()

    def band_lanes(band):
        return slice(band * LANES, (band + 1) * LANES)

    def band_rows(band):
        return slice(band * dates_count, (band + 1) * dates_count)

    def normal_stage(steps, kind):
        arrive(got_m, m_sem.at[kind], steps)
        arrive(got_k, k_sem.at[kind], steps)
        for step in steps:
            tile, columns = tile_at[step], columns_at[step]
            low, high = pair_split(got_k[2 * tile], got_k[2 * tile + 1], half)
            kept_ref[step, 0:GRAM_ROWS] = low
            kept_ref[step, GRAM_ROWS:2 * GRAM_ROWS] = high
            first, second = got_m[2 * tile].astype(jnp.float32), got_m[2 * tile + 1].astype(jnp.float32)
            middle = dates_count // 2
            size = bands_of(first[middle:middle + 1], second[middle:middle + 1], bands, half)
            share = high[GRAM_ROWS - 1:GRAM_ROWS]
            size_ref[step] = jnp.maximum(size * share, SMALLEST) * (1.0 / STEPS)
            low, high = pair_split(first[:middle], second[:middle], half)
            valid_ref[step, 0:middle] = low
            valid_ref[step, middle:dates_count] = high
        kept = jnp.concatenate([kept_ref[step] for step in steps], axis=1)
        weights = jnp.concatenate([valid_ref[step] for step in steps], axis=1).astype(jnp.bfloat16)
        pairs = dot(pair_table, weights)
        size = TERMS * TERMS
        normal = dot(mix_ref[...], jnp.concatenate(three_parts(kept), axis=0).astype(jnp.bfloat16))
        normal = normal + ((pairs[2 * size:] + pairs[size:2 * size]) + pairs[:size])
        wide = lax.broadcasted_iota(jnp.int32, (TERMS, LANES * len(steps)), 0)
        matrix = [
            normal[at * TERMS:(at + 1) * TERMS] + jnp.where(wide == at, RIDGE, 0.0)
            for at in range(TERMS)
        ]
        for pivot in range(TERMS):
            scale = 1.0 / matrix[pivot][pivot:pivot + 1]
            pivot_row = jnp.where(wide == pivot, 1.0, matrix[pivot]) * scale
            for at in range(TERMS):
                if at != pivot:
                    matrix[at] = (
                        jnp.where(wide == pivot, 0.0, matrix[at]) - matrix[at][pivot:pivot + 1] * pivot_row
                    )
            matrix[pivot] = pivot_row
        for place, step in enumerate(steps):
            for at in range(TERMS):
                inverse_ref[step, at] = matrix[at][:, place * LANES:(place + 1) * LANES]
            valid = valid_ref[step]
            entering = x_ref[:, columns_at[step]].astype(jnp.float32)
            observed = jnp.concatenate(
                [entering[band_rows(band)] * valid for band in range(bands)], axis=1
            )
            parts = dot(right_table, observed.astype(jnp.bfloat16))
            right_ref[step] = (parts[2 * TERMS:] + parts[TERMS:2 * TERMS]) + parts[:TERMS]

    def solve(step):
        kept = kept_ref[step]
        weight = row_weight(kept[0:1], kept[GRAM_ROWS + 1:GRAM_ROWS + 2])
        kept_rows = take_steps(got_r, half, tile_at[step]) * size_ref[step][:, None, :] * weight[None]
        solved = []
        for band in range(bands):
            right = (
                right_ref[step, :, band_lanes(band)]
                + kept_rows[band]
            )
            total = None
            for at in range(TERMS):
                term = inverse_ref[step, at] * right[at:at + 1]
                total = term if total is None else total + term
            solved.append(total)
        return solved

    def stacked(solved):
        coefs = jnp.concatenate(solved, axis=1)
        high = narrow(coefs)
        return jnp.concatenate([high, coefs - high, high], axis=0).astype(jnp.bfloat16)

    def misfit_squares(step, parts):
        fitted = dot(enter_table, parts)
        entering = x_ref[:, columns_at[step]].astype(jnp.float32)
        valid = valid_ref[step]
        for band in range(bands):
            misfit = valid * (entering[band_rows(band)] - fitted[:, band_lanes(band)])
            square = misfit * misfit
            total = square[0:TERMS]
            for start in range(TERMS, dates_count, TERMS):
                total = total + square[start:start + TERMS]
            square_ref[band * TERMS:(band + 1) * TERMS] += total

    def leaving_rest(step, parts):
        fitted = dot(leave_table, parts)
        for band in range(bands):
            rest_ref[band_rows(band), columns_at[step]] = (
                old_ref[band_rows(band), columns_at[step]].astype(jnp.float32) - fitted[:, band_lanes(band)]
            )

    def send_coefs(steps, solved_of):
        unit = NEAR if steps[0] in near_steps else far_unit
        for step, solved in zip(steps, solved_of):
            tile = tile_at[step]
            grouped = jnp.concatenate(solved, axis=0).reshape(bands, TERMS, LANES)
            size = half_peaks(jnp.max(jnp.abs(grouped), axis=1), half)
            send_steps(grouped, size, half, send_c, tile)
            sizes = lanes_of(size, half)
            send_u[2 * tile] = sizes
            send_u[2 * tile + 1] = pltpu.roll(sizes, half, 1)
            for peer in peers_of(step):
                remote(send_c, got_c, C_SEND, c_sem.at[unit], peer).start()
                remote(send_u, got_u, U_SEND, u_sem.at[unit], peer).start()

    def send_spread():
        sums = jnp.sum(jnp.sum(square_ref[...].reshape(bands, TERMS, LANES), axis=1), axis=1, keepdims=True)
        lane = lax.broadcasted_iota(jnp.int32, (bands, LANES), 1)
        row = lax.broadcasted_iota(jnp.int32, (bands, LANES), 0)
        local = jnp.sum(jnp.where(lane == row, sums, 0.0), axis=0, keepdims=True)
        send_s[...] = local
        got_s[me] = local
        for step in reversed(range(tiles)):
            for peer in peers_of(step):
                pltpu.make_async_remote_copy(
                    src_ref=send_s,
                    dst_ref=got_s.at[me],
                    send_sem=send_sem.at[S_SEND],
                    recv_sem=s_sem.at[0],
                    device_id={"pix": peer},
                    device_id_type=MESH,
                ).start()

    def solve_steps(unit):
        arrive(got_r, r_sem.at[unit], units[unit])
        solved_of = [solve(step) for step in units[unit]]
        return solved_of, [stacked(solved) for solved in solved_of]

    def per_step(act, steps, values_of):
        for step, values in zip(steps, values_of):
            act(step, values)

    normal_stage(near_steps, 0)
    solved_of, parts_of = solve_steps(NEAR)
    send_coefs(near_steps, solved_of)
    per_step(misfit_squares, near_steps, parts_of)
    per_step(leaving_rest, near_steps, parts_of)
    got_c[me] = send_c[me]
    got_u[me] = send_u[me]
    normal_stage(far_steps, 1)
    far_solved, far_parts = solve_steps(FAR)
    send_coefs(units[FAR][:1], far_solved[:1])
    per_step(misfit_squares, units[FAR], far_parts)
    per_step(leaving_rest, units[FAR], far_parts)
    last_solved, last_parts = solve_steps(LAST)
    per_step(misfit_squares, units[LAST], last_parts)
    send_spread()
    send_coefs(units[FAR][1:] + units[LAST], far_solved[1:] + last_solved)
    per_step(leaving_rest, units[LAST], last_parts)

    for unit in (NEAR, FAR, LAST):
        arrive(got_c, c_sem.at[unit], units[unit])
        arrive(got_u, u_sem.at[unit], units[unit])
        for step in units[unit]:
            tile = tile_at[step]
            size = bands_of(got_u[2 * tile], got_u[2 * tile + 1], bands, half) * (1.0 / STEPS)
            coefs = take_steps(got_c, half, tile) * size[:, None, :]
            coef_out[:, columns_at[step]] = coefs.reshape(width, LANES)

    others = got_s.at[pl.ds(1, owners - 1)]
    pltpu.make_async_copy(others, others, s_sem.at[0]).wait()
    spread = jnp.sum(got_s[...], axis=0) / (dates_count * local_pix * owners)
    inverse_spread = 1.0 / jnp.sqrt(spread + EPSILON)
    lane = lax.broadcasted_iota(jnp.int32, (bands, LANES), 1)
    row = lax.broadcasted_iota(jnp.int32, (bands, LANES), 0)
    scale = jnp.sum(jnp.where(lane == row, inverse_spread, 0.0), axis=1, keepdims=True)
    scale_out[...] = jnp.broadcast_to(scale, (bands, LANES))

    sent(send_m, M_SEND)
    sent(send_k, K_SEND)
    sent(send_r, R_SEND)
    sent(send_c, C_SEND)
    sent(send_u, U_SEND)
    sent(got_s, S_SEND)


def finish_kernel(dates_count, bands, coef_ref, rest_ref, scale_ref, coef_hbm, retired_hbm, retired_ref, sems):
    coef_copy = pltpu.make_async_copy(coef_ref, coef_hbm, sems.at[0])
    coef_copy.start()
    tiles = rest_ref.shape[1] // LANES
    for band in range(bands):
        scale = jnp.broadcast_to(scale_ref[band:band + 1], (dates_count, LANES))
        band_rows = slice(band * dates_count, (band + 1) * dates_count)
        for tile in range(tiles):
            columns = slice(tile * LANES, (tile + 1) * LANES)
            retired_ref[band, :, columns] = (rest_ref[band_rows, columns] * scale).astype(jnp.bfloat16)
        pltpu.make_async_copy(retired_ref.at[band], retired_hbm.at[band], sems.at[1]).start()
    pltpu.make_async_copy(retired_ref, retired_hbm, sems.at[1]).wait()
    coef_copy.wait()


def fused_on_device(new_obs, old_obs, new_mask, new_dates, old_dates, kept_gram, kept_rhs):
    owners = lax.axis_size("pix")
    dates_count, bands, local_pix = new_obs.shape
    rows = dates_count * bands
    width = TERMS * bands
    tiles = local_pix // LANES
    stay = lambda values: pltpu.with_memory_space_constraint(values, pltpu.HBM)
    band_major = lambda values: stay(values.transpose(1, 0, 2).reshape(-1, local_pix))
    hbm = pl.BlockSpec(memory_space=pltpu.HBM)
    vmem = pl.BlockSpec(memory_space=pltpu.VMEM)
    f32, bf16, i16 = jnp.float32, jnp.bfloat16, jnp.int16
    dma = pltpu.SemaphoreType.DMA
    mix = jnp.asarray(gram_mix(), bf16)
    coefs, rest, scale = pl.pallas_call(
        functools.partial(refit_kernel, owners, dates_count, bands, local_pix),
        out_shape=(
            pltpu.VMEM((width, local_pix), f32),
            pltpu.VMEM((rows, local_pix), f32),
            pltpu.VMEM((bands, LANES), f32),
        ),
        in_specs=[hbm] * 8,
        out_specs=(vmem,) * 3,
        scratch_shapes=[
            pltpu.VMEM((2, rows, local_pix), bf16),
            pltpu.VMEM((dates_count, local_pix), jnp.int32),
            pltpu.VMEM((4 * TERMS, local_pix), f32),
            pltpu.VMEM((width, local_pix), f32),
            pltpu.SMEM((dates_count,), jnp.int32),
            pltpu.SMEM((dates_count,), jnp.int32),
            pltpu.VMEM(mix.shape, bf16),
            pltpu.VMEM((owners, dates_count // 2 + 1, LANES), bf16),
            pltpu.VMEM((owners, dates_count // 2 + 1, LANES), bf16),
            pltpu.VMEM((owners, GRAM_ROWS, LANES), f32),
            pltpu.VMEM((owners, GRAM_ROWS, LANES), f32),
            pltpu.VMEM((owners, width // 2, LANES), i16),
            pltpu.VMEM((owners, width // 2, LANES), i16),
            pltpu.VMEM((owners, width // 2, LANES), i16),
            pltpu.VMEM((owners, width // 2, LANES), i16),
            pltpu.VMEM((owners, 1, LANES), f32),
            pltpu.VMEM((owners, 1, LANES), f32),
            pltpu.VMEM((1, LANES), f32),
            pltpu.VMEM((owners, 1, LANES), f32),
            pltpu.VMEM((tiles, dates_count, LANES), f32),
            pltpu.VMEM((tiles, mix.shape[1] // 3, LANES), f32),
            pltpu.VMEM((tiles, bands, LANES), f32),
            pltpu.VMEM((tiles, TERMS, TERMS, LANES), f32),
            pltpu.VMEM((tiles, TERMS, bands * LANES), f32),
            pltpu.VMEM((width, LANES), f32),
            dma((7,)), dma((6,)), dma((2,)), dma((2,)), dma((3,)), dma((3,)), dma((3,)), dma((1,)),
        ],
        compiler_params=pltpu.CompilerParams(
            collective_id=0, has_side_effects=True, vmem_limit_bytes=20 << 20
        ),
    )(
        band_major(new_obs), band_major(old_obs), stay(new_mask), stay(new_dates), stay(old_dates),
        stay(kept_gram), band_major(kept_rhs), stay(mix),
    )
    coefs, retired = pl.pallas_call(
        functools.partial(finish_kernel, dates_count, bands),
        out_shape=(
            jax.ShapeDtypeStruct((width, local_pix), f32),
            jax.ShapeDtypeStruct((bands, dates_count, local_pix), bf16),
        ),
        in_specs=[vmem] * 3,
        out_specs=(hbm, hbm),
        scratch_shapes=[pltpu.VMEM((bands, dates_count, local_pix), bf16), dma((2,))],
        compiler_params=pltpu.CompilerParams(vmem_limit_bytes=4 << 20),
    )(coefs, rest, scale)
    return (
        coefs.reshape(bands, TERMS, local_pix).transpose(1, 0, 2),
        retired.transpose(1, 0, 2),
    )


def on_device(*arrays):
    owners = lax.axis_size("pix")
    dates_count, bands, local_pix = arrays[0].shape
    fits = (
        local_pix == owners * (LANES // 2)
        and owners >= 8
        and owners & (owners - 1) == 0
        and arrays[6].shape[0] == TERMS
        and dates_count % 8 == 0
        and bands % 2 == 0
    )
    return fused_on_device(*arrays) if fits else plain_on_device(*arrays)


def solution(mesh):
    return jax.shard_map(
        on_device,
        mesh=mesh,
        in_specs=(
            P(None, None, ("groups", "pix")),
            P(None, None, ("groups", "pix")),
            P(None, ("groups", "pix")),
            P(),
            P(),
            P(None, ("groups", "pix")),
            P(None, None, ("groups", "pix")),
        ),
        out_specs=(P(None, None, ("groups", "pix")), P(None, None, ("groups", "pix"))),
        check_vma=False,
    )
```

time: 23.3 us -> 22 us (0.944)
  Pallas kernels: 22.5 us -> 21.2 us
    pallas_call x1, Pallas kernels: 21.6 us -> 20.3 us  [fused_on_device(): pl.pallas_call(functools.partial(refit_kernel, owners, dates_count, bands...]
where the time goes in v3:
time: 22 us; the launch traced here: 21.8 us
  Pallas kernels  21.2 us (96%)
  between operations  0.64 us (3%)
    pallas_call x1, Pallas kernels, fused_on_device(): pl.pallas_call(functools.partial(refit_kernel, owners, dates_count, bands...  20.3 us
    pallas_call x1, Pallas kernels, fused_on_device(): pl.pallas_call(functools.partial(finish_kernel, dates_count, bands), out_...  0.89 us

profile of v3, /device:TPU:0, one launch (start us, length us, event | category | flops | bytes accessed | tf_op | source)
XLA Modules:
  0.0 21.8 jit_solution(3282123311695326360)
XLA Ops:
  0.6 20.3 %shard_map.95 = (f32[80,1024]{1,0:T(8,128)S(1)}, f32[240,1024]{1,0:T(8,128)S(1)}, f32[10,128]{1,0:T(8,128)S(1)}) custom-call(bf16[240,1024]{1,0:T(8,128)(2,1)} %bitcast.13, bf16[240,1024]{1,0:T(8,128)(2,1)} %bitcast.14, s32[24,1024]{1,0:T(8,128)} %mask_hbm.1, s32[24]{0:T(128)} %new_dates_hbm.1, s32[24]{0:T(128)} %old_dates_hbm.1, f32[64,1024]{1,0:T(8,128)} %gram_hbm.1, ...), custom_call_target="tpu_custom_call" | custom-call | tf_op jit(solution)/shard_map/pallas_call | solution.py:596
  20.9 0.9 %shard_map.96 = (f32[80,1024]{1,0:T(8,128)}, bf16[10,24,1024]{2,1,0:T(8,128)(2,1)}) custom-call(f32[80,1024]{1,0:T(8,128)S(1)} %get-tuple-element.7.coef_ref, f32[240,1024]{1,0:T(8,128)S(1)} %get-tuple-element.8.rest_ref, f32[10,128]{1,0:T(8,128)S(1)} %get-tuple-element.9.scale_ref), custom_call_target="tpu_custom_call" | custom-call | tf_op jit(solution)/shard_map/pallas_call | solution.py:640

commit v4 on v3

--- a/solution.py
+++ b/solution.py
@@ -240,7 +240,7 @@
     pixels_ref, mask_ref, gram_ref, rhs_ref, new_dates, old_dates, mix_ref,
     send_m, got_m, send_k, got_k, send_r, got_r, send_c, got_c, send_u, got_u, send_s, got_s,
     valid_ref, kept_ref, size_ref, inverse_ref, right_ref, square_ref,
-    load_sem, send_sem, k_sem, m_sem, r_sem, c_sem, u_sem, s_sem,
+    load_sem, send_sem, k_sem, m_sem, r_sem, c_sem, u_sem, s_sem, late_sem,
 ):
     dot = lambda a, b: jnp.dot(a, b, preferred_element_type=jnp.float32)
     me = lax.axis_index("pix")
@@ -282,9 +282,13 @@
         return [2 * tile_at[step], 2 * tile_at[step] + 1]
 
     barrier = pltpu.get_barrier_semaphore()
-    for step in reversed(range(tiles)):
-        for peer in peers_of(step):
-            pl.semaphore_signal(barrier, inc=1, device_id={"pix": peer}, device_id_type=MESH)
+    late = my_tile // (tiles - 1)
+
+    @pl.when(late == 0)
+    def _():
+        for step in reversed(range(tiles)):
+            for peer in peers_of(step):
+                pl.semaphore_signal(barrier, inc=1, device_id={"pix": peer}, device_id_type=MESH)
 
     def load(source, target, at):
         copy = pltpu.make_async_copy(source, target, load_sem.at[at])
@@ -302,6 +306,14 @@
     ]
     load(x_hbm, x_ref, 6)
     load(old_hbm, old_ref, 6)
+
+    @pl.when(late == 1)
+    def _():
+        pl.semaphore_signal(barrier, inc=1, device_id={"pix": flip(me, 1, levels)}, device_id_type=MESH)
+        pl.semaphore_wait(barrier, owners - 1)
+        for step in reversed(range(1, tiles)):
+            for peer in peers_of(step):
+                pl.semaphore_signal(late_sem.at[0], inc=1, device_id={"pix": peer}, device_id_type=MESH)
 
     def remote(source, target, kind, recv, peer):
         return pltpu.make_async_remote_copy(
@@ -348,25 +360,35 @@
         sizes = lanes_of(size, half)
         send_m[2 * tile] = jnp.concatenate([low, sizes], axis=0).astype(jnp.bfloat16)
         send_m[2 * tile + 1] = jnp.concatenate([high, pltpu.roll(sizes, half, 1)], axis=0).astype(jnp.bfloat16)
-    pl.semaphore_wait(barrier, owners - 1)
-
-    def send_normal(steps):
-        kind = int(steps[0] in far_steps)
-        for step in steps:
-            for peer in peers_of(step):
-                remote(send_m, got_m, M_SEND, m_sem.at[kind], peer).start()
-                remote(send_k, got_k, K_SEND, k_sem.at[kind], peer).start()
-
-    def send_right(steps):
-        unit = far_unit if steps[0] in far_steps else NEAR
-        for step in steps:
-            for peer in peers_of(step):
-                remote(send_r, got_r, R_SEND, r_sem.at[unit], peer).start()
-
-    send_normal(far_steps)
-    send_normal(near_steps)
-    send_right(near_steps)
-    send_right(far_steps)
+
+    @pl.when(late == 0)
+    def _():
+        pl.semaphore_wait(barrier, owners - 3)
+
+
+    def send_normal(peers, kind):
+        for peer in peers:
+            remote(send_m, got_m, M_SEND, m_sem.at[kind], peer).start()
+            remote(send_k, got_k, K_SEND, k_sem.at[kind], peer).start()
+
+    def send_right(peers, unit):
+        for peer in peers:
+            remote(send_r, got_r, R_SEND, r_sem.at[unit], peer).start()
+
+    near_peers = [peer for step in near_steps for peer in peers_of(step)]
+    count = len(far_steps)
+    sooner = [my_half * place + (1 - my_half) * (tiles - 2 - place) for place in range(count - 1)]
+    sooner = [2 * tile + core for tile in sooner for core in (0, 1)]
+    later = my_half * (count - 1) + (1 - my_half) * (tiles - 1)
+    later = [2 * later, 2 * later + 1]
+    send_normal(sooner, 1)
+
+    @pl.when((late == 0) & (my_half == 1))
+    def _():
+        pl.semaphore_wait(late_sem.at[0], 2)
+
+    send_normal(near_peers, 0)
+    send_right(near_peers, NEAR)
     got_m[me] = send_m[me]
     got_k[me] = send_k[me]
     got_r[me] = send_r[me]
@@ -384,6 +406,14 @@
     leave_table = fit_rows(old_dates, dates_count).astype(jnp.bfloat16)
     square_ref[...] = jnp.zeros_like(square_ref)
     kept_ref[...] = jnp.zeros_like(kept_ref)
+
+    @pl.when(my_half == 0)
+    def _():
+        pl.semaphore_wait(late_sem.at[0], 2)
+
+    send_normal(later, 1)
+    send_right(sooner, far_unit)
+    send_right(later, far_unit)
     pltpu.make_async_copy(pixels_ref, pixels_ref, load_sem.at[6]).wait()
 
     def band_lanes(band):
@@ -628,7 +658,7 @@
             pltpu.VMEM((tiles, TERMS, TERMS, LANES), f32),
             pltpu.VMEM((tiles, TERMS, bands * LANES), f32),
             pltpu.VMEM((width, LANES), f32),
-            dma((7,)), dma((6,)), dma((2,)), dma((2,)), dma((3,)), dma((3,)), dma((3,)), dma((1,)),
+            dma((7,)), dma((6,)), dma((2,)), dma((2,)), dma((3,)), dma((3,)), dma((3,)), dma((1,)), pltpu.SemaphoreType.REGULAR((1,)),
         ],
         compiler_params=pltpu.CompilerParams(
             collective_id=0, has_side_effects=True, vmem_limit_bytes=20 << 20

time: 22 us -> 20.9 us (0.950)
  Pallas kernels: 21.2 us -> 20.1 us
    pallas_call x1, Pallas kernels: 20.3 us -> 19.2 us  [fused_on_device(): pl.pallas_call(functools.partial(refit_kernel, owners, dates_count, bands...]
where the time goes in v4:
time: 20.9 us; the launch traced here: 20.7 us
  Pallas kernels  20.1 us (96%)
  between operations  0.64 us (3%)
    pallas_call x1, Pallas kernels, fused_on_device(): pl.pallas_call(functools.partial(refit_kernel, owners, dates_count, bands...  19.2 us
    pallas_call x1, Pallas kernels, fused_on_device(): pl.pallas_call(functools.partial(finish_kernel, dates_count, bands), out_...  0.89 us

profile of v4, /device:TPU:0, one launch (start us, length us, event | category | flops | bytes accessed | tf_op | source)
XLA Modules:
  0.0 20.7 jit_solution(797252338377269278)
XLA Ops:
  0.6 19.2 %shard_map.95 = (f32[80,1024]{1,0:T(8,128)S(1)}, f32[240,1024]{1,0:T(8,128)S(1)}, f32[10,128]{1,0:T(8,128)S(1)}) custom-call(bf16[240,1024]{1,0:T(8,128)(2,1)} %bitcast.13, bf16[240,1024]{1,0:T(8,128)(2,1)} %bitcast.14, s32[24,1024]{1,0:T(8,128)} %mask_hbm.1, s32[24]{0:T(128)} %new_dates_hbm.1, s32[24]{0:T(128)} %old_dates_hbm.1, f32[64,1024]{1,0:T(8,128)} %gram_hbm.1, ...), custom_call_target="tpu_custom_call" | custom-call | tf_op jit(solution)/shard_map/pallas_call | solution.py:626
  19.8 0.9 %shard_map.96 = (f32[80,1024]{1,0:T(8,128)}, bf16[10,24,1024]{2,1,0:T(8,128)(2,1)}) custom-call(f32[80,1024]{1,0:T(8,128)S(1)} %get-tuple-element.7.coef_ref, f32[240,1024]{1,0:T(8,128)S(1)} %get-tuple-element.8.rest_ref, f32[10,128]{1,0:T(8,128)S(1)} %get-tuple-element.9.scale_ref), custom_call_target="tpu_custom_call" | custom-call | tf_op jit(solution)/shard_map/pallas_call | solution.py:670

commit v5 on v4

--- a/solution.py
+++ b/solution.py
@@ -199,12 +199,12 @@
 
 
 def send_steps(grouped, size, half, send_ref, tile):
-    steps = jnp.round(grouped * (STEPS / size)[:, None, :])
+    steps = grouped * (STEPS / size)[:, None, :] + (STEPS + 1.5)
     steps = steps.reshape(-1, LANES)
     middle = steps.shape[0] // 2
     low, high = pair_split(steps[:middle], steps[middle:], half)
-    send_ref[2 * tile] = low.astype(jnp.int32).astype(jnp.int16)
-    send_ref[2 * tile + 1] = high.astype(jnp.int32).astype(jnp.int16)
+    send_ref[2 * tile] = (low.astype(jnp.int32) - int(STEPS + 1)).astype(jnp.int16)
+    send_ref[2 * tile + 1] = (high.astype(jnp.int32) - int(STEPS + 1)).astype(jnp.int16)
 
 
 def take_steps(got_ref, half, tile):
@@ -301,11 +301,6 @@
         load(gram_hbm.at[pl.ds(start, count)], gram_ref.at[pl.ds(spot, count)], 1)
         spot += count
     rhs_load = load(rhs_hbm, rhs_ref, 2)
-    table_loads = [
-        load(new_dates_hbm, new_dates, 3), load(old_dates_hbm, old_dates, 4), load(mix_hbm, mix_ref, 5)
-    ]
-    load(x_hbm, x_ref, 6)
-    load(old_hbm, old_ref, 6)
 
     @pl.when(late == 1)
     def _():
@@ -336,6 +331,11 @@
     mask_load.wait()
     pltpu.make_async_copy(gram_ref, gram_ref, load_sem.at[1]).wait()
     rhs_load.wait()
+    table_loads = [
+        load(new_dates_hbm, new_dates, 3), load(old_dates_hbm, old_dates, 4), load(mix_hbm, mix_ref, 5)
+    ]
+    load(x_hbm, x_ref, 6)
+    load(old_hbm, old_ref, 6)
     sub = lax.broadcasted_iota(jnp.int32, (TERMS, LANES), 0)
     for tile in range(tiles):
         columns = slice(tile * LANES, (tile + 1) * LANES)
@@ -346,7 +346,7 @@
         peak = jnp.max(jnp.abs(grouped), axis=1)
         size = narrow(half_peaks(peak, half) * 1.01)
         share = jnp.max(peak / size, axis=0, keepdims=True)
-        send_steps(grouped, jnp.maximum(size * share, SMALLEST), half, send_r, tile)
+        size_ref[tile] = jnp.maximum(size * share, SMALLEST)
         second = jnp.where(sub == 0, pltpu.roll(fourth, 4, 0), second)
         low, high = pair_split(first, second, half)
         send_k[2 * tile, 0:TERMS] = low
@@ -382,6 +382,11 @@
     later = my_half * (count - 1) + (1 - my_half) * (tiles - 1)
     later = [2 * later, 2 * later + 1]
     send_normal(sooner, 1)
+    for tile in range(tiles):
+        columns = slice(tile * LANES, (tile + 1) * LANES)
+        weight = 1.0 / row_weight(gram_ref[0:1, columns], gram_ref[TERMS + 1:TERMS + 2, columns])
+        grouped = rhs_ref[:, columns].reshape(bands, TERMS, LANES) * weight[None]
+        send_steps(grouped, size_ref[tile], half, send_r, tile)
 
     @pl.when((late == 0) & (my_half == 1))
     def _():
@@ -412,8 +417,7 @@
         pl.semaphore_wait(late_sem.at[0], 2)
 
     send_normal(later, 1)
-    send_right(sooner, far_unit)
-    send_right(later, far_unit)
+    send_right([peer for step in far_steps for peer in peers_of(step)], far_unit)
     pltpu.make_async_copy(pixels_ref, pixels_ref, load_sem.at[6]).wait()
 
     def band_lanes(band):
@@ -531,7 +535,7 @@
         local = jnp.sum(jnp.where(lane == row, sums, 0.0), axis=0, keepdims=True)
         send_s[...] = local
         got_s[me] = local
-        for step in reversed(range(tiles)):
+        for step in far_steps + near_steps:
             for peer in peers_of(step):
                 pltpu.make_async_remote_copy(
                     src_ref=send_s,

time: 20.9 us -> 20.6 us (0.986)
  Pallas kernels: 20.1 us -> 19.8 us
    pallas_call x1, Pallas kernels: 19.2 us -> 18.9 us  [fused_on_device(): pl.pallas_call(functools.partial(refit_kernel, owners, dates_count, bands...]
where the time goes in v5:
time: 20.6 us; the launch traced here: 20.5 us
  Pallas kernels  19.8 us (96%)
  between operations  0.64 us (3%)
    pallas_call x1, Pallas kernels, fused_on_device(): pl.pallas_call(functools.partial(refit_kernel, owners, dates_count, bands...  18.9 us
    pallas_call x1, Pallas kernels, fused_on_device(): pl.pallas_call(functools.partial(finish_kernel, dates_count, bands), out_...  0.89 us

profile of v5, /device:TPU:0, one launch (start us, length us, event | category | flops | bytes accessed | tf_op | source)
XLA Modules:
  0.0 20.5 jit_solution(16789604696782370836)
XLA Ops:
  0.6 18.9 %shard_map.95 = (f32[80,1024]{1,0:T(8,128)S(1)}, f32[240,1024]{1,0:T(8,128)S(1)}, f32[10,128]{1,0:T(8,128)S(1)}) custom-call(bf16[240,1024]{1,0:T(8,128)(2,1)} %bitcast.13, bf16[240,1024]{1,0:T(8,128)(2,1)} %bitcast.14, s32[24,1024]{1,0:T(8,128)} %mask_hbm.1, s32[24]{0:T(128)} %new_dates_hbm.1, s32[24]{0:T(128)} %old_dates_hbm.1, f32[64,1024]{1,0:T(8,128)} %gram_hbm.1, ...), custom_call_target="tpu_custom_call" | custom-call | tf_op jit(solution)/shard_map/pallas_call | solution.py:630
  19.6 0.9 %shard_map.96 = (f32[80,1024]{1,0:T(8,128)}, bf16[10,24,1024]{2,1,0:T(8,128)(2,1)}) custom-call(f32[80,1024]{1,0:T(8,128)S(1)} %get-tuple-element.7.coef_ref, f32[240,1024]{1,0:T(8,128)S(1)} %get-tuple-element.8.rest_ref, f32[10,128]{1,0:T(8,128)S(1)} %get-tuple-element.9.scale_ref), custom_call_target="tpu_custom_call" | custom-call | tf_op jit(solution)/shard_map/pallas_call | solution.py:674

commit v6 on v5

--- a/solution.py
+++ b/solution.py
@@ -393,7 +393,6 @@
         pl.semaphore_wait(late_sem.at[0], 2)
 
     send_normal(near_peers, 0)
-    send_right(near_peers, NEAR)
     got_m[me] = send_m[me]
     got_k[me] = send_k[me]
     got_r[me] = send_r[me]
@@ -417,7 +416,8 @@
         pl.semaphore_wait(late_sem.at[0], 2)
 
     send_normal(later, 1)
-    send_right([peer for step in far_steps for peer in peers_of(step)], far_unit)
+    send_right(near_peers, NEAR)
+    send_right([peer for at in [0, 1, 2, 3] for peer in peers_of(far_steps[at])], far_unit)
     pltpu.make_async_copy(pixels_ref, pixels_ref, load_sem.at[6]).wait()
 
     def band_lanes(band):
@@ -556,13 +556,13 @@
             act(step, values)
 
     normal_stage(near_steps, 0)
+    normal_stage(far_steps, 1)
     solved_of, parts_of = solve_steps(NEAR)
     send_coefs(near_steps, solved_of)
     per_step(misfit_squares, near_steps, parts_of)
     per_step(leaving_rest, near_steps, parts_of)
     got_c[me] = send_c[me]
     got_u[me] = send_u[me]
-    normal_stage(far_steps, 1)
     far_solved, far_parts = solve_steps(FAR)
     send_coefs(units[FAR][:1], far_solved[:1])
     per_step(misfit_squares, units[FAR], far_parts)
@@ -570,7 +570,7 @@
     last_solved, last_parts = solve_steps(LAST)
     per_step(misfit_squares, units[LAST], last_parts)
     send_spread()
-    send_coefs(units[FAR][1:] + units[LAST], far_solved[1:] + last_solved)
+    send_coefs(units[FAR][1:] + units[LAST][::-1], far_solved[1:] + last_solved[::-1])
     per_step(leaving_rest, units[LAST], last_parts)
 
     for unit in (NEAR, FAR, LAST):

time: 20.6 us -> 20.4 us (level)
    pallas_call x1, Pallas kernels: 18.9 us -> 18.7 us  [fused_on_device(): pl.pallas_call(functools.partial(refit_kernel, owners, dates_count, bands...]
where the time goes in v6:
time: 20.4 us; the launch traced here: 20.2 us
  Pallas kernels  19.6 us (96%)
  between operations  0.64 us (3%)
    pallas_call x1, Pallas kernels, fused_on_device(): pl.pallas_call(functools.partial(refit_kernel, owners, dates_count, bands...  18.7 us
    pallas_call x1, Pallas kernels, fused_on_device(): pl.pallas_call(functools.partial(finish_kernel, dates_count, bands), out_...  0.89 us

profile of v6, /device:TPU:0, one launch (start us, length us, event | category | flops | bytes accessed | tf_op | source)
XLA Modules:
  0.0 20.2 jit_solution(2168964234171417489)
XLA Ops:
  0.6 18.7 %shard_map.95 = (f32[80,1024]{1,0:T(8,128)S(1)}, f32[240,1024]{1,0:T(8,128)S(1)}, f32[10,128]{1,0:T(8,128)S(1)}) custom-call(bf16[240,1024]{1,0:T(8,128)(2,1)} %bitcast.13, bf16[240,1024]{1,0:T(8,128)(2,1)} %bitcast.14, s32[24,1024]{1,0:T(8,128)} %mask_hbm.1, s32[24]{0:T(128)} %new_dates_hbm.1, s32[24]{0:T(128)} %old_dates_hbm.1, f32[64,1024]{1,0:T(8,128)} %gram_hbm.1, ...), custom_call_target="tpu_custom_call" | custom-call | tf_op jit(solution)/shard_map/pallas_call | solution.py:630
  19.3 0.9 %shard_map.96 = (f32[80,1024]{1,0:T(8,128)}, bf16[10,24,1024]{2,1,0:T(8,128)(2,1)}) custom-call(f32[80,1024]{1,0:T(8,128)S(1)} %get-tuple-element.7.coef_ref, f32[240,1024]{1,0:T(8,128)S(1)} %get-tuple-element.8.rest_ref, f32[10,128]{1,0:T(8,128)S(1)} %get-tuple-element.9.scale_ref), custom_call_target="tpu_custom_call" | custom-call | tf_op jit(solution)/shard_map/pallas_call | solution.py:674
